TPU v7x, 512 devices: a whole 4x8x8 slice. The times are simulated.
512 devices in a mesh: gx: 8 (over y_lo, x), gy: 4 (over y_hi), gz: 16 (over z, core).
Axes of the slice: x: 4, y: 8 (y_hi: 4, y_lo: 2; y = y_hi * 2 + y_lo), z: 8, core: 2. Of those that a mesh axis runs over, the one named last changes fastest.
Arguments:
- source_term: float32 [64, 64, 2048], P('gx', 'gy', 'gz'), may hold values from -6 to 6
- conductivity: float32 [64, 64, 2048], P('gx', 'gy', 'gz'), may hold values from 0.3 to 3
- initial_guess: float32 [64, 64, 2048], P('gx', 'gy', 'gz'), may hold values from -4 to 4
- box_owner: int32 [8, 4, 16], replicated, may hold values from 0 to 3
Outputs:
- potential: float32 [64, 64, 2048], P('gx', 'gy', 'gz')
Inputs may be any that keep to these rules, and one draw needn't show every extreme that they name: `box_owner`: labels of the coarse boxes; boxes with equal labels couple only within one plane of boxes along z.
All inputs are finite; a program needn't handle non-finite values.
Results may differ from a plain program's by a relative error of at most 0.0001.
Values sent between devices are 32-bit elements; how exact they have to be, the bound alone decides.
A program may use at most 64 MiB of HBM per device.

v0:
```python
import jax
import jax.numpy as jnp
from jax import lax
from jax.sharding import PartitionSpec as P

CSWEEPS = 8


screening = 0.05


def with_halo(block, sides, width):
    for axis, dim in sides:
        count = lax.axis_size(axis)
        forward = [(i, i + 1) for i in range(count - 1)]
        forward.append((count - 1, 0))
        backward = [(target, source) for source, target in forward]
        low = lax.ppermute(
            lax.slice_in_dim(block, block.shape[dim] - width, None, axis=dim), axis, forward
        )
        high = lax.ppermute(lax.slice_in_dim(block, 0, width, axis=dim), axis, backward)
        block = jnp.concatenate([low, block, high], axis=dim)
    return block


def coarsen(values):
    extent = values.shape
    return values.reshape(extent[0] // 2, 2, extent[1] // 2, 2, extent[2] // 2, 2).mean(
        axis=(1, 3, 5)
    )


def refine(values):
    return jnp.repeat(jnp.repeat(jnp.repeat(values, 2, 0), 2, 1), 2, 2)


def trimmed(values, margin):
    return values[margin:-margin, margin:-margin, margin:-margin]


def weights_from(padded, stiffness):
    centre = padded[1:-1, 1:-1, 1:-1]
    weights = (
        (centre + padded[2:, 1:-1, 1:-1]) * 0.5,
        (centre + padded[:-2, 1:-1, 1:-1]) * 0.5,
        (centre + padded[1:-1, 2:, 1:-1]) * 0.5,
        (centre + padded[1:-1, :-2, 1:-1]) * 0.5,
        (centre + padded[1:-1, 1:-1, 2:]) * 0.5,
        (centre + padded[1:-1, 1:-1, :-2]) * 0.5,
    )
    diagonal = screening + stiffness * (
        weights[0] + weights[1] + weights[2] + weights[3] + weights[4] + weights[5]
    )
    return (weights, diagonal)


def neighbour_sum(padded, weights, margin):
    parts = [trimmed(values, margin) for values in weights]
    return (
        parts[0] * padded[2:, 1:-1, 1:-1]
        + parts[1] * padded[:-2, 1:-1, 1:-1]
        + parts[2] * padded[1:-1, 2:, 1:-1]
        + parts[3] * padded[1:-1, :-2, 1:-1]
        + parts[4] * padded[1:-1, 1:-1, 2:]
        + parts[5] * padded[1:-1, 1:-1, :-2]
    )


def relax_cells(padded, depth, level_data, colour):
    weights, diagonal, source_ext, parity_ext, stiffness = level_data
    margin = 2 - depth
    centre = padded[1:-1, 1:-1, 1:-1]
    nearby = neighbour_sum(padded, weights, margin)
    updated = (trimmed(source_ext, margin) + stiffness * nearby) / trimmed(diagonal, margin)
    return jnp.where(trimmed(parity_ext, margin) == colour, updated, centre)


def smooth(field, level_data):
    for colour in (0, 1):
        padded = with_halo(field, (("gx", 0), ("gy", 1), ("gz", 2)), 1)
        field = relax_cells(padded, 1, level_data, colour)
    return field


def level_setup(coef, source, stiffness):
    coef_ext = jnp.pad(with_halo(coef, (("gx", 0), ("gy", 1), ("gz", 2)), 1), 1)
    source_ext = jnp.pad(source, 1)
    weights, diagonal = weights_from(coef_ext, stiffness)
    extent = source.shape
    x_index = jnp.arange(extent[0] + 2, dtype=jnp.int32) + lax.axis_index("gx") * extent[0] - 1
    y_index = jnp.arange(extent[1] + 2, dtype=jnp.int32) + lax.axis_index("gy") * extent[1] - 1
    z_index = jnp.arange(extent[2] + 2, dtype=jnp.int32) + lax.axis_index("gz") * extent[2] - 1
    parity_ext = (x_index[:, None, None] + y_index[None, :, None] + z_index[None, None, :]) % 2
    return (weights, diagonal, source_ext, parity_ext, stiffness)


def beside_all(field, weights):
    return (
        weights[0] * jnp.roll(field, -1, 0)
        + weights[1] * jnp.roll(field, 1, 0)
        + weights[2] * jnp.roll(field, -1, 1)
        + weights[3] * jnp.roll(field, 1, 1)
        + weights[4] * jnp.roll(field, -1, 2)
        + weights[5] * jnp.roll(field, 1, 2)
    )


def coarse_solve(source, diagonal, weights, labels, box_depth, stiffness):
    extent = source.shape
    z_local = jnp.arange(extent[2], dtype=jnp.int32) % box_depth
    z_up = jnp.broadcast_to((z_local != box_depth - 1)[None, None, :], extent)
    z_down = jnp.broadcast_to((z_local != 0)[None, None, :], extent)
    masks = (
        labels == jnp.roll(labels, -1, 0),
        labels == jnp.roll(labels, 1, 0),
        labels == jnp.roll(labels, -1, 1),
        labels == jnp.roll(labels, 1, 1),
        z_up,
        z_down,
    )
    cut_weights = tuple((weights[index] * masks[index].astype(jnp.float32) for index in range(6)))
    x_index = jnp.arange(extent[0], dtype=jnp.int32)
    y_index = jnp.arange(extent[1], dtype=jnp.int32)
    z_index = jnp.arange(extent[2], dtype=jnp.int32)
    parity = (x_index[:, None, None] + y_index[None, :, None] + z_index[None, None, :]) % 2
    correction = jnp.zeros(extent, jnp.float32)
    for _ in range(CSWEEPS):
        for colour in (0, 1):
            updated = (source + stiffness * beside_all(correction, cut_weights)) / diagonal
            correction = jnp.where(parity == colour, updated, correction)
    return correction


def assemble(gathered, boxes_x, boxes_y, boxes_z, box_extent):
    width_x, width_y, width_z = box_extent
    blocks = gathered.reshape(boxes_x, boxes_y, boxes_z, 8, width_x, width_y, width_z)
    blocks = blocks.transpose(3, 0, 4, 1, 5, 2, 6)
    return blocks.reshape(8, boxes_x * width_x, boxes_y * width_y, boxes_z * width_z)


def local(source_term, conductivity, initial_guess, box_owner):
    field = initial_guess
    source = source_term
    coef = conductivity
    saved = []
    for coarse_step in range(3):
        stiffness = 0.25**coarse_step
        level_data = level_setup(coef, source, stiffness)
        if coarse_step > 0:
            field = jnp.zeros(source.shape, jnp.float32)
        field = smooth(field, level_data)
        padded = with_halo(field, (("gx", 0), ("gy", 1), ("gz", 2)), 1)
        nearby = neighbour_sum(padded, level_data[0], 1)
        residual = source - (trimmed(level_data[1], 1) * field - stiffness * nearby)
        saved.append((field, level_data))
        source = coarsen(residual)
        coef = coarsen(coef)
    stiffness = 0.25**3
    coef_ext = with_halo(coef, (("gx", 0), ("gy", 1), ("gz", 2)), 1)
    weights, diagonal = weights_from(coef_ext, stiffness)
    box_extent = source.shape
    payload = jnp.stack((source, diagonal) + weights).reshape(
        1, 8, box_extent[0] * box_extent[1] * box_extent[2]
    )
    boxes_x = lax.axis_size("gx")
    boxes_y = lax.axis_size("gy")
    plane_index = lax.axis_index("gz")
    gathered = lax.all_gather(payload, ("gx", "gy", "gz"), axis=0, tiled=True)
    fields = assemble(gathered, boxes_x, boxes_y, lax.axis_size("gz"), box_extent)
    z_start = plane_index * box_extent[2]
    labels = jnp.repeat(
        jnp.repeat(jnp.repeat(box_owner, box_extent[0], 0), box_extent[1], 1), box_extent[2], 2
    )
    correction_all = coarse_solve(
        fields[0],
        fields[1],
        tuple((fields[index] for index in range(2, 8))),
        labels,
        box_extent[2],
        stiffness,
    )
    starts = (lax.axis_index("gx") * box_extent[0], lax.axis_index("gy") * box_extent[1], z_start)
    correction = lax.dynamic_slice(correction_all, starts, box_extent)
    for coarse_step in (2, 1, 0):
        field, level_data = saved[coarse_step]
        field = smooth(field + refine(correction), level_data)
        correction = field
    return correction


def solution(mesh):
    return jax.shard_map(
        local,
        mesh=mesh,
        in_specs=(P("gx", "gy", "gz"), P("gx", "gy", "gz"), P("gx", "gy", "gz"), P()),
        out_specs=P("gx", "gy", "gz"),
        check_vma=False,
    )
```

profile of v0, /device:TPU:1, one launch (start us, length us, event | category | flops | bytes accessed | tf_op | source)
XLA Modules:
  0.0 1303.9 jit_solution(13660067413614063454)
XLA Ops:
  0.0 6.4 collective-permute-start.30
  8.3 6.3 reshape.307
  20.0 5.5 collective-permute-start.72
  25.5 3.4 collective-permute-start.54
  39.7 3.4 collective-permute-start.48
  48.1 5.5 collective-permute-start.6
  55.5 5.5 collective-permute-start.25
  63.0 5.5 collective-permute-start.1
  68.5 4.2 collective-permute-start.33
  74.9 3.8 collective-permute-start.32
  80.2 4.5 collective-permute-start.26
  86.6 3.8 collective-permute-start.74
  92.8 5.0 collective-permute-start.56
  97.9 4.1 collective-permute-start.3
  104.1 5.3 collective-permute-start.8
  111.5 9.8 collective-permute-start.5
  121.2 7.5 collective-permute-start.4
  138.5 3.4 collective-permute-start.13
  141.9 4.1 collective-permute-start.27
  152.2 3.3 collective-permute-done.15
  156.4 3.7 collective-permute-start.16
  161.0 4.7 collective-permute-start.29
  166.6 3.7 collective-permute-start.18
  172.4 4.5 collective-permute-done.19
  178.9 4.1 collective-permute-start.21
  189.7 3.9 collective-permute-start.22
  196.7 4.5 collective-permute-start.51
  201.5 5.6 reshape.306
  212.3 3.4 collective-permute-start.37
  218.8 4.4 collective-permute-start.39
  232.4 3.4 collective-permute-start.40
  242.3 3.2 collective-permute-start.43
  245.6 4.5 collective-permute-start.53
  250.9 4.8 collective-permute-start.45
  255.8 4.8 collective-permute-start.44
  261.7 5.1 collective-permute-start.46
  273.5 3.4 collective-permute-start.61
  280.0 5.3 collective-permute-start.62
  287.5 4.1 collective-permute-start.76
  300.3 3.4 collective-permute-start.67
  308.8 4.2 collective-permute-start.69
  321.7 685.4 %all_gather.3 = f32[512,8,32]{2,1,0:T(8,128)S(1)} all-gather(f32[1,8,32]{2,1,0:T(8,128)S(1)} %stack.32), channel_id=1, replica_groups=mesh['gx'=8,'gy'=4,'gz'=16] {'gx','gy','gz'}, dimensions={0}, use_global_device_ids=true | all-gather | bytes 525312 | tf_op jit(solution)/shard_map/all_gather | solution.py:168
  1007.8 4.3 reshape.309
  1012.1 4.7 fusion.419
  1040.7 3.4 collective-permute-start.79
  1049.1 4.3 collective-permute-start.81
  1055.6 3.9 collective-permute-start.83
  1062.9 11.7 collective-permute-start.84
  1076.5 107.1 %collective-permute-done.85 = f32[1,4,32]{2,1,0:T(4,128)S(1)} collective-permute-done((f32[1,4,32]{2,1,0:T(4,128)S(1)}, f32[1,4,32]{2,1,0:T(4,128)S(1)}, u32[]{:S(2)}, u32[]{:S(2)}) %collective-permute-start.85) | collective-permute-done | bytes 544 | tf_op jit(solution)/shard_map/ppermute | solution.py:18
  1185.6 4.3 collective-permute-start.87
  1197.7 3.6 collective-permute-start.90
  1203.3 4.5 collective-permute-done.91
  1207.8 3.3 collective-permute-start.93
  1211.2 4.1 collective-permute-start.92
  1218.3 4.2 collective-permute-start.94
  1225.9 3.4 collective-permute-start.97
  1232.4 5.8 collective-permute-start.99
  1240.1 3.3 collective-permute-done.98
  1243.5 6.4 collective-permute-start.100
  1253.7 3.4 collective-permute-start.103
  1266.4 3.4 collective-permute-done.105
  1270.0 4.8 collective-permute-start.107
  1281.3 3.4 collective-permute-start.109
  1289.8 4.3 collective-permute-start.111
  (636 shorter events, 225.5 us)
Async XLA Ops:
  0.0 55.5 %collective-permute-start.30 = (f32[1,8,64]{2,1,0:T(8,128)S(1)}, f32[1,8,64]{2,1,0:T(8,128)S(1)}, u32[]{:S(2)}, u32[]{:S(2)}) collective-permute-start(f32[1,8,64]{2,1,0:T(8,128)S(1)} %broadcast.418), channel_id=1, source_target_pairs={{64,0},{128,64},{192,128},{256,192},{320,256},{384,320},{448,384},... | collective-permute-start | bytes 6152 | tf_op jit(solution)/shard_map/ppermute | solution.py:21
  6.4 54.6 %collective-permute-start.31 = (f32[1,8,64]{2,1,0:T(8,128)S(1)}, f32[1,8,64]{2,1,0:T(8,128)S(1)}, u32[]{:S(2)}, u32[]{:S(2)}) collective-permute-start(f32[1,8,64]{2,1,0:T(8,128)S(1)} %broadcast.418), channel_id=1, source_target_pairs={{0,64},{64,128},{128,192},{192,256},{256,320},{320,384},{384,448},... | collective-permute-start | bytes 6152 | tf_op jit(solution)/shard_map/ppermute | solution.py:18
  18.1 19.6 %collective-permute-start.73 = (f32[1,2,16]{2,1,0:T(2,128)S(1)}, f32[1,2,16]{2,1,0:T(2,128)S(1)}, u32[]{:S(2)}, u32[]{:S(2)}) collective-permute-start(f32[1,2,16]{2,1,0:T(2,128)S(1)} %multiply_bitcast_fusion), channel_id=1, source_target_pairs={{0,64},{64,128},{128,192},{192,256},{256,320},{320,384},{384,448},... | collective-permute-start | bytes 392 | tf_op jit(solution)/shard_map/ppermute | solution.py:18
  20.0 19.6 %collective-permute-start.72 = (f32[1,2,16]{2,1,0:T(2,128)S(1)}, f32[1,2,16]{2,1,0:T(2,128)S(1)}, u32[]{:S(2)}, u32[]{:S(2)}) collective-permute-start(f32[1,2,16]{2,1,0:T(2,128)S(1)} %multiply_bitcast_fusion), channel_id=1, source_target_pairs={{64,0},{128,64},{192,128},{256,192},{320,256},{384,320},{448,384},... | collective-permute-start | bytes 392 | tf_op jit(solution)/shard_map/ppermute | solution.py:21
  25.5 22.5 %collective-permute-start.54 = (f32[1,4,32]{2,1,0:T(4,128)S(1)}, f32[1,4,32]{2,1,0:T(4,128)S(1)}, u32[]{:S(2)}, u32[]{:S(2)}) collective-permute-start(f32[1,4,32]{2,1,0:T(4,128)S(1)} %broadcast.427), channel_id=1, source_target_pairs={{64,0},{128,64},{192,128},{256,192},{320,256},{384,320},{448,384},... | collective-permute-start | bytes 1544 | tf_op jit(solution)/shard_map/ppermute | solution.py:21
  39.7 6.4 collective-permute-start.48
  43.1 10.5 collective-permute-start.55
  46.1 51.7 %collective-permute-start.7 = (f32[1,16,128]{2,1,0:T(8,128)S(1)}, f32[1,16,128]{2,1,0:T(8,128)S(1)}, u32[]{:S(2)}, u32[]{:S(2)}) collective-permute-start(f32[1,16,128]{2,1,0:T(8,128)S(1)} %get-tuple-element.272), channel_id=1, source_target_pairs={{0,64},{64,128},{128,192},{192,256},{256,320},{320,384},{384,448},... | collective-permute-start | bytes 24584 | tf_op jit(solution)/shard_map/ppermute | solution.py:18
  48.1 53.9 %collective-permute-start.6 = (f32[1,16,128]{2,1,0:T(8,128)S(1)}, f32[1,16,128]{2,1,0:T(8,128)S(1)}, u32[]{:S(2)}, u32[]{:S(2)}) collective-permute-start(f32[1,16,128]{2,1,0:T(8,128)S(1)} %get-tuple-element.271), channel_id=1, source_target_pairs={{64,0},{128,64},{192,128},{256,192},{320,256},{384,320},{448,384},... | collective-permute-start | bytes 24584 | tf_op jit(solution)/shard_map/ppermute | solution.py:21
  53.5 36.8 %collective-permute-start = (f32[1,16,128]{2,1,0:T(8,128)S(1)}, f32[1,16,128]{2,1,0:T(8,128)S(1)}, u32[]{:S(2)}, u32[]{:S(2)}) collective-permute-start(f32[1,16,128]{2,1,0:T(8,128)S(1)} %get-tuple-element.270), channel_id=1, source_target_pairs={{0,64},{64,128},{128,192},{192,256},{256,320},{320,384},{384,448},... | collective-permute-start | bytes 24584 | tf_op jit(solution)/shard_map/ppermute | solution.py:18
  55.5 7.5 collective-permute-start.25
  61.0 7.5 collective-permute-start.24
  63.0 29.8 %collective-permute-start.1 = (f32[1,16,128]{2,1,0:T(8,128)S(1)}, f32[1,16,128]{2,1,0:T(8,128)S(1)}, u32[]{:S(2)}, u32[]{:S(2)}) collective-permute-start(f32[1,16,128]{2,1,0:T(8,128)S(1)} %get-tuple-element.269), channel_id=1, source_target_pairs={{64,0},{128,64},{192,128},{256,192},{320,256},{384,320},{448,384},... | collective-permute-start | bytes 24584 | tf_op jit(solution)/shard_map/ppermute | solution.py:21
  68.5 6.5 collective-permute-start.33
  80.2 6.4 collective-permute-start.26
  86.6 190.3 %collective-permute-start.74 = (f32[3,1,16]{2,1,0:T(1,128)S(1)}, f32[3,1,16]{2,1,0:T(1,128)S(1)}, u32[]{:S(2)}, u32[]{:S(2)}) collective-permute-start(f32[3,1,16]{2,1,0:T(1,128)S(1)} %get-tuple-element.374), channel_id=1, source_target_pairs={{16,0},{32,16},{48,32},{0,48},{17,1},{33,17},{49,33},{1,49},{18,2}... | collective-permute-start | bytes 584 | tf_op jit(solution)/shard_map/ppermute | solution.py:21
  90.4 186.5 %collective-permute-start.75 = (f32[3,1,16]{2,1,0:T(1,128)S(1)}, f32[3,1,16]{2,1,0:T(1,128)S(1)}, u32[]{:S(2)}, u32[]{:S(2)}) collective-permute-start(f32[3,1,16]{2,1,0:T(1,128)S(1)} %get-tuple-element.373), channel_id=1, source_target_pairs={{0,16},{16,32},{32,48},{48,0},{1,17},{17,33},{33,49},{49,1},{2,18}... | collective-permute-start | bytes 584 | tf_op jit(solution)/shard_map/ppermute | solution.py:18
  92.8 117.5 %collective-permute-start.56 = (f32[4,1,32]{2,1,0:T(1,128)S(1)}, f32[4,1,32]{2,1,0:T(1,128)S(1)}, u32[]{:S(2)}, u32[]{:S(2)}) collective-permute-start(f32[4,1,32]{2,1,0:T(1,128)S(1)} %get-tuple-element.358), channel_id=1, source_target_pairs={{16,0},{32,16},{48,32},{0,48},{17,1},{33,17},{49,33},{1,49},{18,2}... | collective-permute-start | bytes 1544 | tf_op jit(solution)/shard_map/ppermute | solution.py:21
  102.0 7.5 collective-permute-start.2
  104.1 7.3 collective-permute-start.8
  109.4 11.8 collective-permute-start.9
  111.5 17.4 %collective-permute-start.5 = (f32[10,18,1]{2,1,0:T(8,128)S(1)}, f32[10,18,1]{2,1,0:T(8,128)S(1)}, u32[]{:S(2)}, u32[]{:S(2)}) collective-permute-start(f32[10,18,1]{2,1,0:T(8,128)S(1)} %get-tuple-element.62), channel_id=1, source_target_pairs={{1,0},{2,1},{3,2},{4,3},{5,4},{6,5},{7,6},{8,7},{9,8},{10,9},{11,1... | collective-permute-start | bytes 2168 | tf_op jit(solution)/shard_map/ppermute | solution.py:21
  121.2 9.4 collective-permute-start.4
  138.5 7.5 collective-permute-start.13
  141.9 7.2 collective-permute-start.27
  149.1 6.5 collective-permute-start.15
  156.4 9.2 collective-permute-start.16
  170.3 6.5 collective-permute-start.19
  176.8 6.4 collective-permute-start.20
  178.9 7.1 collective-permute-start.21
  186.8 6.9 collective-permute-start.23
  189.7 7.0 collective-permute-start.22
  193.7 18.5 %collective-permute-start.57 = (f32[4,1,32]{2,1,0:T(1,128)S(1)}, f32[4,1,32]{2,1,0:T(1,128)S(1)}, u32[]{:S(2)}, u32[]{:S(2)}) collective-permute-start(f32[4,1,32]{2,1,0:T(1,128)S(1)} %get-tuple-element.357), channel_id=1, source_target_pairs={{0,16},{16,32},{32,48},{48,0},{1,17},{17,33},{33,49},{49,1},{2,18}... | collective-permute-start | bytes 1544 | tf_op jit(solution)/shard_map/ppermute | solution.py:18
  196.7 35.7 %collective-permute-start.51 = (f32[4,1,32]{2,1,0:T(1,128)S(1)}, f32[4,1,32]{2,1,0:T(1,128)S(1)}, u32[]{:S(2)}, u32[]{:S(2)}) collective-permute-start(f32[4,1,32]{2,1,0:T(1,128)S(1)} %get-tuple-element.356), channel_id=1, source_target_pairs={{16,0},{32,16},{48,32},{0,48},{17,1},{33,17},{49,33},{1,49},{18,2}... | collective-permute-start | bytes 1544 | tf_op jit(solution)/shard_map/ppermute | solution.py:21
  212.3 6.5 collective-permute-start.37
  215.7 20.1 %collective-permute-start.50 = (f32[4,1,32]{2,1,0:T(1,128)S(1)}, f32[4,1,32]{2,1,0:T(1,128)S(1)}, u32[]{:S(2)}, u32[]{:S(2)}) collective-permute-start(f32[4,1,32]{2,1,0:T(1,128)S(1)} %get-tuple-element.355), channel_id=1, source_target_pairs={{0,16},{16,32},{32,48},{48,0},{1,17},{17,33},{33,49},{49,1},{2,18}... | collective-permute-start | bytes 1544 | tf_op jit(solution)/shard_map/ppermute | solution.py:18
  218.8 6.5 collective-permute-start.39
  230.4 40.4 %collective-permute-start.59 = (f32[4,6,1]{2,1,0:T(8,128)S(1)}, f32[4,6,1]{2,1,0:T(8,128)S(1)}, u32[]{:S(2)}, u32[]{:S(2)}) collective-permute-start(f32[4,6,1]{2,1,0:T(8,128)S(1)} %get-tuple-element.342), channel_id=1, source_target_pairs={{0,1},{1,2},{2,3},{3,4},{4,5},{5,6},{6,7},{7,8},{8,9},{9,10},{10,1... | collective-permute-start | bytes 296 | tf_op jit(solution)/shard_map/ppermute | solution.py:18
  242.3 7.7 collective-permute-start.43
  250.9 9.7 collective-permute-start.45
  273.5 6.4 collective-permute-start.61
  280.0 11.6 collective-permute-start.62
  285.3 6.4 collective-permute-start.63
  287.5 16.2 %collective-permute-start.76 = (f32[3,4,1]{2,1,0:T(4,128)S(1)}, f32[3,4,1]{2,1,0:T(4,128)S(1)}, u32[]{:S(2)}, u32[]{:S(2)}) collective-permute-start(f32[3,4,1]{2,1,0:T(4,128)S(1)} %get-tuple-element.360), channel_id=1, source_target_pairs={{1,0},{2,1},{3,2},{4,3},{5,4},{6,5},{7,6},{8,7},{9,8},{10,9},{11,1... | collective-permute-start | bytes 152 | tf_op jit(solution)/shard_map/ppermute | solution.py:21
  291.6 12.1 collective-permute-start.77
  300.3 6.4 collective-permute-start.67
  306.7 6.6 collective-permute-start.68
  308.8 6.4 collective-permute-start.69
  1040.7 6.4 collective-permute-start.79
  1049.1 6.4 collective-permute-start.81
  1062.9 13.7 %collective-permute-start.84 = (f32[1,4,32]{2,1,0:T(4,128)S(1)}, f32[1,4,32]{2,1,0:T(4,128)S(1)}, u32[]{:S(2)}, u32[]{:S(2)}) collective-permute-start(f32[1,4,32]{2,1,0:T(4,128)S(1)} %get-tuple-element.362), channel_id=1, source_target_pairs={{64,0},{128,64},{192,128},{256,192},{320,256},{384,320},{448,384},... | collective-permute-start | bytes 1544 | tf_op jit(solution)/shard_map/ppermute | solution.py:21
  1074.6 109.1 %collective-permute-start.85 = (f32[1,4,32]{2,1,0:T(4,128)S(1)}, f32[1,4,32]{2,1,0:T(4,128)S(1)}, u32[]{:S(2)}, u32[]{:S(2)}) collective-permute-start(f32[1,4,32]{2,1,0:T(4,128)S(1)} %get-tuple-element.361), channel_id=1, source_target_pairs={{0,64},{64,128},{128,192},{192,256},{256,320},{320,384},{384,448},... | collective-permute-start | bytes 1544 | tf_op jit(solution)/shard_map/ppermute | solution.py:18
  1185.6 6.4 collective-permute-start.87
  1201.3 6.5 collective-permute-start.91
  1207.8 7.4 collective-permute-start.93
  1211.2 7.0 collective-permute-start.92
  1225.9 6.5 collective-permute-start.97
  1232.4 7.7 collective-permute-start.99
  1243.5 7.2 collective-permute-start.100
  1253.7 6.5 collective-permute-start.103
  1263.4 6.5 collective-permute-start.105
  1270.0 6.8 collective-permute-start.107
  1281.3 6.5 collective-permute-start.109
  1289.8 6.5 collective-permute-start.111
  (113 other events, 6296.1 us)
where the time goes:
time: 1310 us; the launch traced here: 1300 us
  blocking collectives  685 us (52%)
  starting transfers between devices  349 us (27%)
  waiting for transfers between devices  197 us (15%)
  local copies, waits for them, and re-layouts  49 us (4%)
  other arithmetic  20.5 us (2%)
    all_gather x1, blocking collectives, local(): gathered = lax.all_gather(payload, ('gx', 'gy', 'gz'), axis=0, tiled=True)  685 us
    ppermute x57, starting transfers between devices, with_halo(): lax.ppermute(lax.slice_in_dim(block, 0, width, axis=dim), axis, backward)  201 us
    ppermute x57, waiting for transfers between devices, with_halo(): lax.ppermute(lax.slice_in_dim(block, block.shape[dim] - width, None, axis...  171 us
    ppermute x57, starting transfers between devices, with_halo(): lax.ppermute(lax.slice_in_dim(block, block.shape[dim] - width, None, axis...  148 us
  transfers between devices with their start and end apart: 114, of which 50 were waited for; matrix products, arithmetic and copies ran while one was open for 3% of the time, Pallas kernels for 0%

commit v1 on v0

v1 whole, which is shorter than its diff:
```python
import itertools

import jax
import jax.numpy as jnp
from jax import lax
from jax.experimental import pallas as pl
from jax.experimental.pallas import tpu as pltpu
from jax.sharding import PartitionSpec as P

MESH = pl.DeviceIdType.MESH
SX, SY, SZ = 8, 4, 16
CSWEEPS = 8
screening = 0.05

NEAR = [d for d in itertools.product((-1, 0, 1), repeat=3) if d != (0, 0, 0)]
CLOSE = [d for d in NEAR if abs(d[0]) + abs(d[1]) + abs(d[2]) <= 2]
PLANE = [d for d in itertools.product(range(SX), range(SY)) if d != (0, 0)]
ALONG = [-2, -1, 1, 2]


def everyone():
    found = {(a % SX, b % SY, c % SZ) for a, b, c in NEAR}
    found |= {(a, b, 0) for a, b in PLANE}
    found |= {(0, 0, c % SZ) for c in ALONG}
    return sorted(found)


def roll(values, shift, axis):
    shift = shift % values.shape[axis]
    return values if shift == 0 else pltpu.roll(values, shift, axis)


def around(before, here, after, step):
    return (
        after,
        before,
        roll(here, -1, 0),
        roll(here, 1, 0),
        roll(here, -step, 1),
        roll(here, step, 1),
    )


def faces(before, here, after, step, stiffness):
    half = 0.5 * stiffness
    weights = [half * (here + other) for other in around(before, here, after, step)]
    diagonal = screening + (
        (weights[0] + weights[1]) + (weights[2] + weights[3]) + (weights[4] + weights[5])
    )
    return weights, diagonal


def relaxed(level, scaled, before, here, after, step):
    sides = around(before, here, after, step)
    terms = [scaled[n] * sides[n] for n in range(6)]
    return level + (((terms[0] + terms[1]) + (terms[2] + terms[3])) + (terms[4] + terms[5]))


def pair_sum(values):
    lane = lax.broadcasted_iota(jnp.int32, values.shape, len(values.shape) - 1)
    return values + jnp.where(lane % 2 == 0, roll(values, -1, 1), roll(values, 1, 1))


def kernel(
    f_in, c_in, v_in, owner, out,
    E0, PK0, PZ0, A0, D0, U0, PKV, PZV, R0,
    E1, PK1, PZ1, A1, D1, V1, X1, R1,
    T2, ZR, S2, W2, V2, A2, D2, R2, E3, A3, B3,
    in_sem, a_s, a_r, c1_s, c1_r, b1_s, b1_r, v0_s, v0_r, z_s, z_r, m_s, m_r,
):
    me = (lax.axis_index("gx"), lax.axis_index("gy"), lax.axis_index("gz"))

    def at(d):
        return tuple(
            lax.rem(me[i] + d[i] + size, size) for i, size in enumerate((SX, SY, SZ))
        )

    def send(src, dst, send_sem, recv_sem, d):
        copy = pltpu.make_async_remote_copy(
            src_ref=src, dst_ref=dst, send_sem=send_sem, recv_sem=recv_sem,
            device_id=at(d), device_id_type=MESH,
        )
        copy.start()
        return copy

    loads = [
        pltpu.make_async_copy(ref, E0.at[pl.ds(3, 8), n, pl.ds(0, 16), pl.ds(0, 128)], in_sem.at[n])
        for n, ref in enumerate((v_in, c_in, f_in))
    ]
    for copy in loads:
        copy.start()
    barrier = pltpu.get_barrier_semaphore()
    others = everyone()
    for d in others:
        pl.semaphore_signal(barrier, inc=1, device_id=at(d), device_id_type=MESH)
    for copy in loads:
        copy.wait()

    lane16 = lax.broadcasted_iota(jnp.int32, (16, 128), 1)
    packed = jnp.zeros((16, 128), jnp.float32)
    for i in range(8):
        for n in range(3):
            lo, count = (16 * i + 6 * n, 6) if n < 2 else (16 * i + 12, 4)
            moved = roll(E0[3 + i, n, 0:16, 0:128], lo - (125 if n < 2 else 126), 1)
            packed = jnp.where((lane16 >= lo) & (lane16 < lo + count), moved, packed)
    PK0[...] = packed

    def coarsen0(get, store):
        for i in range(4):
            R0[i] = pair_sum(get(2 * i) + get(2 * i + 1))
        for i in range(4):
            store(i, 0.125 * (R0[i, pl.ds(0, 8, stride=2), :] + R0[i, pl.ds(1, 8, stride=2), :]))

    lane8 = lax.broadcasted_iota(jnp.int32, (8, 128), 1)

    def pack1(kind):
        tile = jnp.zeros((8, 128), jnp.float32)
        for i in range(4):
            moved = roll(E1[4 + i, kind, 0:8, 0:128], 16 * i - 120, 1)
            tile = jnp.where((lane8 >= 16 * i) & (lane8 < 16 * i + 16), moved, tile)
        PK1[kind] = tile

    row_of = lax.broadcasted_iota(jnp.int32, (128, 128), 0)
    col_of = lax.broadcasted_iota(jnp.int32, (128, 128), 1)
    squeeze = jnp.where(row_of // 4 == (col_of + 16) % 32, 0.25, 0.0).astype(jnp.float32)

    def coarsen1(get, kind):
        both = jnp.concatenate([get(0) + get(1), get(2) + get(3)], axis=0)
        R1[...] = jnp.dot(
            both, squeeze, precision=lax.Precision.HIGHEST, preferred_element_type=jnp.float32
        )
        T2[kind] = 0.25 * (R1[pl.ds(0, 8, stride=2), :] + R1[pl.ds(1, 8, stride=2), :])

    def put_c1(i, value):
        E1[4 + i, 0, 0:8, 0:128] = value

    coarsen0(lambda i: E0[3 + i, 1, 0:16, 0:128], put_c1)
    pack1(0)
    coarsen1(lambda i: E1[4 + i, 0, 0:8, 0:128], 0)

    pl.semaphore_wait(barrier, len(others))

    x_from = {0: (3, 8), 1: (8, 3), -1: (3, 3)}
    x_to = {0: (3, 8), 1: (0, 3), -1: (11, 3)}
    y_from = {0: (0, 16), 1: (13, 3), -1: (0, 3)}
    y_to = {0: (0, 16), 1: (21, 3), -1: (16, 3)}
    lanes = pl.ds(0, 128)

    def side_of(oz):
        return 0 if oz == -1 else 1

    copies_a = []
    for k, (ox, oy, oz) in enumerate(NEAR):
        if oz == 0:
            src = E0.at[pl.ds(*x_from[ox]), :, pl.ds(*y_from[oy]), lanes]
            dst = E0.at[pl.ds(*x_to[ox]), :, pl.ds(*y_to[oy]), lanes]
        else:
            src = PK0.at[pl.ds(*y_from[oy])]
            dst = PZ0.at[side_of(oz), 1 - ox, pl.ds(*y_to[oy])]
        copies_a.append(send(src, dst, a_s.at[k], a_r.at[k], (ox, oy, oz)))

    def swap1(kind, send_sem, recv_sem):
        xd = {0: 4, 1: 0, -1: 8}
        ys = {0: (0, 8), 1: (4, 4), -1: (0, 4)}
        yd = {0: (0, 8), 1: (12, 4), -1: (8, 4)}
        copies = []
        for k, (ox, oy, oz) in enumerate(NEAR):
            if oz == 0:
                src = E1.at[pl.ds(4, 4), kind, pl.ds(*ys[oy]), lanes]
                dst = E1.at[pl.ds(xd[ox], 4), kind, pl.ds(*yd[oy]), lanes]
            else:
                src = PK1.at[kind, pl.ds(*ys[oy])]
                dst = PZ1.at[kind, side_of(oz), 1 - ox, pl.ds(*yd[oy])]
            copies.append(send(src, dst, send_sem.at[k], recv_sem.at[k], (ox, oy, oz)))
        return copies

    def stage_z(kind):
        return [
            send(T2.at[kind], ZR.at[kind, k], z_s.at[kind, k], z_r.at[kind, k], (0, 0, oz))
            for k, oz in enumerate(ALONG)
        ]

    def window(kind):
        ahead2, ahead1, behind1, behind2 = (ZR[kind, k] for k in range(4))
        tile = jnp.where(lane8 < 16, behind2, behind1)
        tile = jnp.where(lane8 < 48, tile, T2[kind])
        tile = jnp.where(lane8 < 80, tile, ahead1)
        tile = jnp.where(lane8 < 112, tile, ahead2)
        for i in range(2):
            S2[kind, i, 0:4] = tile[4 * i : 4 * i + 4]
            W2[kind, i, 0:4] = tile[4 * i : 4 * i + 4]

    def stage_xy(kind):
        copies = []
        for k, (ox, oy) in enumerate(PLANE):
            dx, dy = (SX - ox) % SX, (SY - oy) % SY
            src = S2.at[kind, :, pl.ds(0, 4)]
            dst = W2.at[kind, pl.ds(2 * dx, 2), pl.ds(4 * dy, 4)]
            copies.append(send(src, dst, m_s.at[kind, k], m_r.at[kind, k], (ox, oy, 0)))
        return copies

    copies_c1 = swap1(0, c1_s, c1_r)
    copies_cz = stage_z(0)

    sub8 = lax.broadcasted_iota(jnp.int32, (8, 128), 0)
    labels = []
    for x in range(SX):
        bx = lax.rem(me[0] + x, SX)
        tile = jnp.zeros((8, 128), jnp.int32)
        for y in range(SY):
            by = lax.rem(me[1] + y, SY)
            low, mid, high = (
                owner[bx, by, lax.rem(me[2] + dz + SZ, SZ)] for dz in (-1, 0, 1)
            )
            part = jnp.where(lane8 < 48, low, jnp.where(lane8 < 80, mid, high))
            tile = jnp.where(sub8 // 2 == y, part, tile)
        labels.append(tile)

    for copy in copies_a:
        copy.wait_recv()
    for copy in copies_a:
        copy.wait_send()

    lane24 = lax.broadcasted_iota(jnp.int32, (24, 128), 1)
    slot = lane24 % 16
    from_below = (slot < 3) | ((slot >= 6) & (slot < 9)) | ((slot >= 12) & (slot < 14))
    for dx in range(3):
        both = jnp.where(from_below, PZ0[1, dx], PZ0[0, dx])
        for p in {0: range(0, 3), 1: range(3, 11), 2: range(11, 14)}[dx]:
            i = {0: p + 5, 1: p - 3, 2: p - 11}[dx]
            for n in range(3):
                lo, base = (16 * i + 6 * n, 125) if n < 2 else (16 * i + 12, 126)
                E0[p, n, :, 128:256] = roll(both, base - lo, 1)

    shape0 = (24, 256)
    par0 = (lax.broadcasted_iota(jnp.int32, shape0, 0) + lax.broadcasted_iota(jnp.int32, shape0, 1)) % 2

    def setup0(p, carry):
        weights, diagonal = faces(E0[p - 1, 1], E0[p, 1], E0[p + 1, 1], 1, 1.0)
        inverse = 1.0 / diagonal
        for n in range(6):
            A0[p, n] = weights[n] * inverse
        A0[p, 6] = E0[p, 2] * inverse
        D0[p] = diagonal
        return carry

    lax.fori_loop(1, 13, setup0, 0)

    def point_v(p):
        scaled = [A0[p, n] for n in range(6)]
        here = E0[p, 0]
        update = relaxed(A0[p, 6], scaled, E0[p - 1, 0], here, E0[p + 1, 0], 1)
        return update, here

    def pass_v(q):
        def body(p, carry):
            update, here = point_v(p)
            E0[p, 0] = jnp.where(par0 == (p + 1 + q) % 2, update, here)
            return carry
        return body

    lax.fori_loop(1, 13, pass_v(0), 0)
    lax.fori_loop(2, 12, pass_v(1), 0)

    packed = jnp.zeros((16, 128), jnp.float32)
    for i in range(8):
        moved = roll(E0[3 + i, 0, 0:16, 0:128], 16 * i - 126, 1)
        packed = jnp.where((lane16 >= 16 * i) & (lane16 < 16 * i + 4), moved, packed)
    PKV[...] = packed

    def resid0(i):
        update, here = point_v(3 + i)
        return (D0[3 + i] * (update - here))[0:16, 0:128]

    for copy in copies_c1:
        copy.wait_recv()

    def unpack1(kind):
        lane_16 = lax.broadcasted_iota(jnp.int32, (16, 128), 1)
        for dx in range(3):
            both = jnp.where(lane_16 % 16 < 8, PZ1[kind, 1, dx], PZ1[kind, 0, dx])
            for i in range(4):
                E1[4 * dx + i, kind, :, 128:256] = roll(both, 120 - 16 * i, 1)

    unpack1(0)

    def setup1(p, carry):
        weights, diagonal = faces(E1[p - 1, 0], E1[p, 0], E1[p + 1, 0], 2, 0.25)
        inverse = 1.0 / diagonal
        for n in range(6):
            A1[p, n] = weights[n] * inverse
        A1[p, 6] = inverse
        D1[p] = diagonal
        return carry

    lax.fori_loop(1, 11, setup1, 0)

    def put_b1(i, value):
        E1[4 + i, 1, 0:8, 0:128] = value * A1[4 + i, 6, 0:8, 0:128]

    coarsen0(resid0, put_b1)
    pack1(1)
    for copy in copies_c1:
        copy.wait_send()
    copies_b1 = swap1(1, b1_s, b1_r)

    xs = {0: (3, 8), 1: (9, 2), -1: (3, 2)}
    xd = {0: (2, 8), 1: (0, 2), -1: (10, 2)}
    ys = {0: (0, 16), 1: (14, 2), -1: (0, 2)}
    yd = {0: (0, 16), 1: (22, 2), -1: (16, 2)}
    copies_v0 = []
    for k, (ox, oy, oz) in enumerate(CLOSE):
        if oz == 0:
            src = E0.at[pl.ds(*xs[ox]), 0, pl.ds(*ys[oy]), lanes]
            dst = U0.at[pl.ds(*xd[ox]), pl.ds(*yd[oy]), lanes]
        else:
            src = PKV.at[pl.ds(*ys[oy])]
            dst = PZV.at[side_of(oz), 1 - ox, pl.ds(*yd[oy])]
        copies_v0.append(send(src, dst, v0_s.at[k], v0_r.at[k], (ox, oy, oz)))
    for i in range(8):
        U0[2 + i, 0:16, 0:128] = E0[3 + i, 0, 0:16, 0:128]

    for copy in copies_cz:
        copy.wait_recv()
    window(0)
    copies_cm = stage_xy(0)

    for copy in copies_b1:
        copy.wait_recv()

    unpack1(1)
    shape1 = (16, 256)
    par1 = (
        lax.broadcasted_iota(jnp.int32, shape1, 0) + lax.broadcasted_iota(jnp.int32, shape1, 1) // 2
    ) % 2
    for p in range(12):
        V1[p] = jnp.where(par1 == p % 2, E1[p, 1], 0.0)

    def point1(p):
        scaled = [A1[p, n] for n in range(6)]
        here = V1[p]
        return relaxed(E1[p, 1], scaled, V1[p - 1], here, V1[p + 1], 2), here

    def pass1(q):
        def body(p, carry):
            update, here = point1(p)
            V1[p] = jnp.where(par1 == (p + q) % 2, update, here)
            return carry
        return body

    lax.fori_loop(1, 11, pass1(1), 0)

    def resid1(i):
        update, here = point1(4 + i)
        return (D1[4 + i] * (update - here))[0:8, 0:128]

    coarsen1(resid1, 1)
    copies_fz = stage_z(1)

    for copy in copies_cm:
        copy.wait_recv()

    def setup2(p, carry):
        here = W2[0, p]
        weights, diagonal = faces(
            W2[0, lax.rem(p + 15, 16)], here, W2[0, lax.rem(p + 1, 16)], 1, 0.0625
        )
        inverse = 1.0 / diagonal
        for n in range(6):
            A2[p, n] = weights[n] * inverse
        A2[p, 6] = inverse
        D2[p] = diagonal
        return carry

    def coarsen2(get, store):
        for i in range(8):
            R2[i] = pair_sum(get(2 * i) + get(2 * i + 1))
        for i in range(8):
            store(i, 0.125 * (R2[i, pl.ds(0, 8, stride=2), :] + R2[i, pl.ds(1, 8, stride=2), :]))

    def put_c3(i, value):
        E3[i] = value

    for copy in copies_fz:
        copy.wait_recv()
    window(1)
    copies_fm = stage_xy(1)

    lax.fori_loop(0, 16, setup2, 0)
    coarsen2(lambda i: W2[0, i], put_c3)
    z3 = ((lane8 + 16) % 32) // 2
    for x in range(8):
        weights, diagonal = faces(E3[(x + 7) % 8], E3[x], E3[(x + 1) % 8], 2, 0.015625)
        inverse = 1.0 / diagonal
        label = labels[x]
        joined = (
            label == labels[(x + 1) % 8],
            label == labels[(x + 7) % 8],
            label == roll(label, -1, 0),
            label == roll(label, 1, 0),
            z3 != 15,
            z3 != 0,
        )
        for n in range(6):
            A3[x, n] = jnp.where(joined[n], weights[n] * inverse, 0.0)
        B3[x] = inverse

    for copy in copies_fm:
        copy.wait_recv()

    shape2 = (16, 128)
    par2 = (
        lax.broadcasted_iota(jnp.int32, shape2, 0) + lax.broadcasted_iota(jnp.int32, shape2, 1)
    ) % 2
    for p in range(16):
        W2[1, p] = W2[1, p] * A2[p, 6]
        V2[p] = jnp.where(par2 == p % 2, W2[1, p], 0.0)

    def point2(p):
        scaled = [A2[p, n] for n in range(6)]
        here = V2[p]
        before, after = V2[lax.rem(p + 15, 16)], V2[lax.rem(p + 1, 16)]
        return relaxed(W2[1, p], scaled, before, here, after, 1), here

    def pass2(q, start):
        def body(t, carry):
            p = lax.rem(t + start, 16)
            update, here = point2(p)
            V2[p] = jnp.where(par2 == (p + q) % 2, update, here)
            return carry
        return body

    lax.fori_loop(0, 16, pass2(1, 0), 0)

    def resid2(p):
        update, here = point2(p)
        return D2[p] * (update - here)

    def put_b3(i, value):
        B3[i] = value * B3[i]

    coarsen2(resid2, put_b3)

    par3 = (sub8 + lane8 // 2 + me[0]) % 2
    for x in range(8):
        E3[x] = jnp.where(par3 == x % 2, B3[x], 0.0)

    def pass3(q):
        for x in range(8):
            scaled = [A3[x, n] for n in range(6)]
            here = E3[x]
            update = relaxed(B3[x], scaled, E3[(x + 7) % 8], here, E3[(x + 1) % 8], 2)
            E3[x] = jnp.where(par3 == (x + q) % 2, update, here)

    pass3(1)

    def sweep3(t, carry):
        pass3(0)
        pass3(1)
        return carry

    lax.fori_loop(0, CSWEEPS - 1, sweep3, 0)

    for p in range(16):
        R2[p // 2, pl.ds(0, 8, stride=2), :] = E3[p // 2]
        R2[p // 2, pl.ds(1, 8, stride=2), :] = E3[p // 2]
    for p in range(16):
        V2[p] = V2[p] + R2[p // 2]
    lax.fori_loop(0, 8, pass2(0, 13), 0)
    lax.fori_loop(0, 6, pass2(1, 14), 0)

    wide_row = lax.broadcasted_iota(jnp.int32, (128, 256), 0)
    wide_col = lax.broadcasted_iota(jnp.int32, (128, 256), 1)
    beyond = wide_col - 128
    origin = jnp.where(
        wide_col < 128,
        48 + wide_col // 4,
        jnp.where(beyond < 64, 80 + beyond // 4, 16 + beyond // 4),
    )
    stretch = jnp.where(wide_row == origin, 1.0, 0.0).astype(jnp.float32)
    pieces = []
    for x in range(-2, 4):
        plane = V2[x % 16]
        pieces.append(jnp.where(sub8 < 6, plane[0:8], plane[8:16]))
    spread = jnp.dot(
        jnp.concatenate(pieces, axis=0), stretch,
        precision=lax.Precision.HIGHEST, preferred_element_type=jnp.float32,
    )
    for x in range(6):
        part = spread[8 * x : 8 * x + 8]
        for half in range(2):
            piece = part[:, 128 * half : 128 * half + 128]
            X1[x, half, pl.ds(0, 8, stride=2), :] = piece
            X1[x, half, pl.ds(1, 8, stride=2), :] = piece
    for p in range(1, 11):
        x = p - 4
        add = jnp.concatenate([X1[x // 2 + 2, 0], X1[x // 2 + 2, 1]], axis=1)
        V1[p] = V1[p] + add
    lax.fori_loop(2, 10, pass1(0), 0)
    lax.fori_loop(3, 9, pass1(1), 0)

    for copy in copies_v0:
        copy.wait_recv()
    for dx in range(3):
        both = jnp.where(lane24 % 16 < 2, PZV[1, dx], PZV[0, dx])
        for p in {0: range(0, 2), 1: range(2, 10), 2: range(10, 12)}[dx]:
            i = {0: p + 6, 1: p - 2, 2: p - 10}[dx]
            U0[p, :, 128:256] = roll(both, 126 - 16 * i, 1)
    sub256 = lax.broadcasted_iota(jnp.int32, (8, 256), 0)
    for j in range(6):
        value = V1[3 + j]
        for half in range(2):
            piece = value[0:8, 128 * half : 128 * half + 128]
            R0[half, pl.ds(0, 8, stride=2), :] = piece
            R0[half, pl.ds(1, 8, stride=2), :] = piece
        inner = jnp.concatenate([R0[0], R0[1]], axis=1)
        outer = jnp.where(
            sub256 < 4,
            jnp.broadcast_to(value[8:9], (8, 256)),
            jnp.broadcast_to(value[15:16], (8, 256)),
        )
        add = jnp.concatenate([inner, outer], axis=0)
        U0[2 * j] = U0[2 * j] + add
        U0[2 * j + 1] = U0[2 * j + 1] + add

    def point_u(p):
        scaled = [A0[p + 1, n] for n in range(6)]
        here = U0[p]
        return relaxed(A0[p + 1, 6], scaled, U0[p - 1], here, U0[p + 1], 1), here

    def up0(p, carry):
        update, here = point_u(p)
        U0[p] = jnp.where(par0 == p % 2, update, here)
        return carry

    lax.fori_loop(1, 11, up0, 0)

    def last0(p, carry):
        update, here = point_u(p)
        out[p - 2] = jnp.where(par0 == (p + 1) % 2, update, here)[0:16, 0:128]
        return carry

    lax.fori_loop(2, 10, last0, 0)

    for copies in (copies_cz, copies_b1, copies_v0, copies_cm, copies_fz, copies_fm):
        for copy in copies:
            copy.wait_send()


def local(source_term, conductivity, initial_guess, box_owner):
    def vmem(*shape):
        return pltpu.VMEM(shape, jnp.float32)

    dma = pltpu.SemaphoreType.DMA
    scratch = [
        vmem(14, 3, 24, 256), vmem(16, 128), vmem(2, 3, 24, 128), vmem(14, 7, 24, 256),
        vmem(14, 24, 256), vmem(12, 24, 256), vmem(16, 128), vmem(2, 3, 24, 128), vmem(4, 16, 128),
        vmem(12, 2, 16, 256), vmem(2, 8, 128), vmem(2, 2, 3, 16, 128), vmem(12, 7, 16, 256),
        vmem(12, 16, 256), vmem(12, 16, 256), vmem(6, 2, 16, 128), vmem(16, 128),
        vmem(2, 8, 128), vmem(2, 4, 8, 128), vmem(2, 2, 8, 128), vmem(2, 16, 16, 128),
        vmem(16, 16, 128), vmem(16, 7, 16, 128), vmem(16, 16, 128), vmem(8, 16, 128),
        vmem(8, 8, 128), vmem(8, 6, 8, 128), vmem(8, 8, 128),
        dma((3,)), dma((26,)), dma((26,)), dma((26,)), dma((26,)), dma((26,)), dma((26,)),
        dma((18,)), dma((18,)), dma((2, 4)), dma((2, 4)), dma((2, 31)), dma((2, 31)),
    ]
    anywhere = pl.BlockSpec(memory_space=pl.ANY)
    return pl.pallas_call(
        kernel,
        out_shape=jax.ShapeDtypeStruct(source_term.shape, jnp.float32),
        in_specs=[anywhere, anywhere, anywhere, pl.BlockSpec(memory_space=pltpu.SMEM)],
        out_specs=pl.BlockSpec(memory_space=pltpu.VMEM),
        scratch_shapes=scratch,
        compiler_params=pltpu.CompilerParams(
            collective_id=0, has_side_effects=True, vmem_limit_bytes=40 << 20
        ),
    )(source_term, conductivity, initial_guess, box_owner)


def solution(mesh):
    return jax.shard_map(
        local,
        mesh=mesh,
        in_specs=(P("gx", "gy", "gz"), P("gx", "gy", "gz"), P("gx", "gy", "gz"), P()),
        out_specs=P("gx", "gy", "gz"),
        check_vma=False,
    )
```

time: 1310 us -> 62.4 us (0.05)
  blocking collectives: 685 us -> 0 us
  starting transfers between devices: 349 us -> 0 us
  waiting for transfers between devices: 197 us -> 0 us
  Pallas kernels: 0 us -> 58.2 us
  local copies, waits for them, and re-layouts: 49 us -> 3.87 us
  other arithmetic: 20.5 us -> 0 us
    all_gather x1 -> x0, blocking collectives: 685 us -> none  [local(): gathered = lax.all_gather(payload, ('gx', 'gy', 'gz'), axis=0, tiled=True)]
    ppermute x114 -> x0, starting transfers between devices: 349 us -> none  [the longest x57 201 us: with_halo(): lax.ppermute(lax.slice_in_dim(block, 0, width, axis=dim), axis, backward)]
    ppermute x114 -> x0, waiting for transfers between devices: 197 us -> none  [the longest x57 171 us: with_halo(): lax.ppermute(lax.slice_in_dim(block, block.shape[dim] - width, None, axis...]
    pallas_call x0 -> x1, Pallas kernels: none -> 58.2 us  [local(): pl.pallas_call(kernel, out_shape=jax.ShapeDtypeStruct(source_term.shape,...]
    slice x151 -> x0, local copies, waits for them, and re-layouts: 19.8 us -> none  [the longest x7 8.1 us: local(): fields[index]]
    reshape x9 -> x0, local copies, waits for them, and re-layouts: 17.5 us -> none  [the longest x3 12.5 us: coarsen(): values.reshape(extent[0] // 2, 2, extent[1] // 2, 2, extent[2] // 2, 2)]
  transfers between devices with their start and end apart: 114 -> 0, of which waited for: 50 -> 0; matrix products, arithmetic and copies ran while one was open for 3% -> 0% of each run, Pallas kernels for 0% -> 0%
where the time goes in v1:
time: 62.4 us; the launch traced here: 62.1 us
  Pallas kernels  58.2 us (93%)
  local copies, waits for them, and re-layouts  3.87 us (6%)
    pallas_call x1, Pallas kernels, local(): pl.pallas_call(kernel, out_shape=jax.ShapeDtypeStruct(source_term.shape,...  58.2 us
    unnamed x9, local copies, waits for them, and re-layouts  3.87 us

profile of v1, /device:TPU:1, one launch (start us, length us, event | category | flops | bytes accessed | tf_op | source)
XLA Modules:
  0.0 62.1 jit_solution(12212673252701952511)
XLA Ops:
  0.0 0.0 copy-start
  0.0 0.8 %copy-done = f32[8,16,128]{2,1,0:T(8,128)S(1)} copy-done((f32[8,16,128]{2,1,0:T(8,128)S(1)}, f32[8,16,128]{2,1,0:T(8,128)}, u32[]{:S(2)}) %copy-start) | copy-done | bytes 65560
  0.8 0.0 copy-start.1
  0.8 0.8 %copy-done.1 = f32[8,16,128]{2,1,0:T(8,128)S(1)} copy-done((f32[8,16,128]{2,1,0:T(8,128)S(1)}, f32[8,16,128]{2,1,0:T(8,128)}, u32[]{:S(2)}) %copy-start.1) | copy-done | bytes 65560
  1.7 0.0 copy-start.2
  1.7 0.8 %copy-done.2 = f32[8,16,128]{2,1,0:T(8,128)S(1)} copy-done((f32[8,16,128]{2,1,0:T(8,128)S(1)}, f32[8,16,128]{2,1,0:T(8,128)}, u32[]{:S(2)}) %copy-start.2) | copy-done | bytes 65560
  2.5 0.0 copy-start.3
  2.5 0.7 %copy-done.3 = s32[8,4,16]{2,1,0:T(4,128)S(1)} copy-done((s32[8,4,16]{2,1,0:T(4,128)S(1)}, s32[8,4,16]{2,1,0:T(4,128)}, u32[]{:S(2)}) %copy-start.3) | copy-done | bytes 2072
  3.2 58.2 %shard_map.46 = f32[8,16,128]{2,1,0:T(8,128)S(1)} custom-call(f32[8,16,128]{2,1,0:T(8,128)S(1)} %copy-done, f32[8,16,128]{2,1,0:T(8,128)S(1)} %copy-done.1, f32[8,16,128]{2,1,0:T(8,128)S(1)} %copy-done.2, s32[8,4,16]{2,1,0:T(4,128)S(1)} %copy-done.3), custom_call_target="tpu_custom_call" | custom-call | tf_op jit(solution)/shard_map/pallas_call | solution.py:567
  61.5 0.6 %copy.6 = f32[8,16,128]{2,1,0:T(8,128)} copy(f32[8,16,128]{2,1,0:T(8,128)S(1)} %shard_map.46) | data formatting | bytes 131072
Async XLA Ops:
  0.0 0.8 %copy-start = (f32[8,16,128]{2,1,0:T(8,128)S(1)}, f32[8,16,128]{2,1,0:T(8,128)}, u32[]{:S(2)}) copy-start(f32[8,16,128]{2,1,0:T(8,128)} %f_in.1) | copy-start | bytes 196612
  0.8 0.8 %copy-start.1 = (f32[8,16,128]{2,1,0:T(8,128)S(1)}, f32[8,16,128]{2,1,0:T(8,128)}, u32[]{:S(2)}) copy-start(f32[8,16,128]{2,1,0:T(8,128)} %c_in.1) | copy-start | bytes 196612
  1.7 0.8 %copy-start.2 = (f32[8,16,128]{2,1,0:T(8,128)S(1)}, f32[8,16,128]{2,1,0:T(8,128)}, u32[]{:S(2)}) copy-start(f32[8,16,128]{2,1,0:T(8,128)} %v_in.1) | copy-start | bytes 196612
  2.5 0.7 %copy-start.3 = (s32[8,4,16]{2,1,0:T(4,128)S(1)}, s32[8,4,16]{2,1,0:T(4,128)}, u32[]{:S(2)}) copy-start(s32[8,4,16]{2,1,0:T(4,128)} %owner.1) | copy-start | bytes 6148

commit v2 on v1

--- a/solution.py
+++ b/solution.py
@@ -56,16 +56,30 @@
     return level + (((terms[0] + terms[1]) + (terms[2] + terms[3])) + (terms[4] + terms[5]))
 
 
+def beyond_block(x, count):
+    return max(0, -x, x - count + 1)
+
+
+def quarters(away, reach, rows, all_rows):
+    inner = (slice(0, rows), slice(0, 128))
+    found = [inner]
+    if away + 1 <= reach:
+        found += [(slice(rows, all_rows), slice(0, 128)), (slice(0, rows), slice(128, 256))]
+    if away + 2 <= reach:
+        found.append((slice(rows, all_rows), slice(128, 256)))
+    return found
+
+
 def pair_sum(values):
     lane = lax.broadcasted_iota(jnp.int32, values.shape, len(values.shape) - 1)
     return values + jnp.where(lane % 2 == 0, roll(values, -1, 1), roll(values, 1, 1))
 
 
 def kernel(
-    f_in, c_in, v_in, owner, out,
-    E0, PK0, PZ0, A0, D0, U0, PKV, PZV, R0,
-    E1, PK1, PZ1, A1, D1, V1, X1, R1,
-    T2, ZR, S2, W2, V2, A2, D2, R2, E3, A3, B3,
+    f_in, c_in, v_in, owner_in, out,
+    E0, PK0, PZ0, A0, D0, VA, VB, U0, UA, UB, PKV, PZV, R0, X0,
+    E1, PK1, PZ1, A1, D1, V1, V1B, V1C, V1D, X1, R1,
+    T2, ZR, S2, W2, V2, V2B, V2C, A2, D2, R2, E3, A3, B3, owner,
     in_sem, a_s, a_r, c1_s, c1_r, b1_s, b1_r, v0_s, v0_r, z_s, z_r, m_s, m_r,
 ):
     me = (lax.axis_index("gx"), lax.axis_index("gy"), lax.axis_index("gz"))
@@ -87,6 +101,7 @@
         pltpu.make_async_copy(ref, E0.at[pl.ds(3, 8), n, pl.ds(0, 16), pl.ds(0, 128)], in_sem.at[n])
         for n, ref in enumerate((v_in, c_in, f_in))
     ]
+    loads.append(pltpu.make_async_copy(owner_in, owner, in_sem.at[3]))
     for copy in loads:
         copy.start()
     barrier = pltpu.get_barrier_semaphore()
@@ -218,8 +233,6 @@
 
     for copy in copies_a:
         copy.wait_recv()
-    for copy in copies_a:
-        copy.wait_send()
 
     lane24 = lax.broadcasted_iota(jnp.int32, (24, 128), 1)
     slot = lane24 % 16
@@ -235,42 +248,50 @@
     shape0 = (24, 256)
     par0 = (lax.broadcasted_iota(jnp.int32, shape0, 0) + lax.broadcasted_iota(jnp.int32, shape0, 1)) % 2
 
-    def setup0(p, carry):
+    for p in range(1, 13):
         weights, diagonal = faces(E0[p - 1, 1], E0[p, 1], E0[p + 1, 1], 1, 1.0)
         inverse = 1.0 / diagonal
-        for n in range(6):
-            A0[p, n] = weights[n] * inverse
-        A0[p, 6] = E0[p, 2] * inverse
-        D0[p] = diagonal
-        return carry
-
-    lax.fori_loop(1, 13, setup0, 0)
-
-    def point_v(p):
+        level = E0[p, 2] * inverse
+        for rows, cols in quarters(beyond_block(p - 3, 8), 2, 16, 24):
+            for n in range(6):
+                A0[p, n, rows, cols] = (weights[n] * inverse)[rows, cols]
+            A0[p, 6, rows, cols] = level[rows, cols]
+        if 3 <= p < 11:
+            D0[p - 3] = diagonal[0:16, 0:128]
+
+    def point0(get, p):
         scaled = [A0[p, n] for n in range(6)]
-        here = E0[p, 0]
-        update = relaxed(A0[p, 6], scaled, E0[p - 1, 0], here, E0[p + 1, 0], 1)
-        return update, here
-
-    def pass_v(q):
-        def body(p, carry):
-            update, here = point_v(p)
-            E0[p, 0] = jnp.where(par0 == (p + 1 + q) % 2, update, here)
-            return carry
-        return body
-
-    lax.fori_loop(1, 13, pass_v(0), 0)
-    lax.fori_loop(2, 12, pass_v(1), 0)
-
-    packed = jnp.zeros((16, 128), jnp.float32)
-    for i in range(8):
-        moved = roll(E0[3 + i, 0, 0:16, 0:128], 16 * i - 126, 1)
-        packed = jnp.where((lane16 >= 16 * i) & (lane16 < 16 * i + 4), moved, packed)
-    PKV[...] = packed
+        here = get(p)
+        return relaxed(A0[p, 6], scaled, get(p - 1), here, get(p + 1), 1), here
+
+    def colour0(get, store, planes, q, reach):
+        for p in planes:
+            update, here = point0(get, p)
+            mixed = jnp.where(par0 == (p + 1 + q) % 2, update, here)
+            for rows, cols in quarters(beyond_block(p - 3, 8), reach, 16, 24):
+                store(p, rows, cols, mixed[rows, cols])
+
+    def get_e(p):
+        return E0[p, 0]
+
+    def get_va(p):
+        return VA[p - 1]
+
+    def put_va(p, rows, cols, value):
+        VA[p - 1, rows, cols] = value
+
+    def get_vb(p):
+        return VB[p - 2]
+
+    def put_vb(p, rows, cols, value):
+        VB[p - 2, rows, cols] = value
+
+    colour0(get_e, put_va, range(1, 13), 0, 2)
+    colour0(get_va, put_vb, range(2, 12), 1, 1)
 
     def resid0(i):
-        update, here = point_v(3 + i)
-        return (D0[3 + i] * (update - here))[0:16, 0:128]
+        update, here = point0(get_vb, 3 + i)
+        return D0[i] * (update - here)[0:16, 0:128]
 
     for copy in copies_c1:
         copy.wait_recv()
@@ -284,41 +305,48 @@
 
     unpack1(0)
 
-    def setup1(p, carry):
+    def setup1(p):
         weights, diagonal = faces(E1[p - 1, 0], E1[p, 0], E1[p + 1, 0], 2, 0.25)
         inverse = 1.0 / diagonal
         for n in range(6):
             A1[p, n] = weights[n] * inverse
-        A1[p, 6] = inverse
-        D1[p] = diagonal
-        return carry
-
-    lax.fori_loop(1, 11, setup1, 0)
+        if 4 <= p < 8:
+            D1[p - 4] = diagonal[0:8, 0:128]
+
+    own1 = []
+    for p in range(4, 8):
+        own1.append(1.0 / faces(E1[p - 1, 0], E1[p, 0], E1[p + 1, 0], 2, 0.25)[1][0:8, 0:128])
 
     def put_b1(i, value):
-        E1[4 + i, 1, 0:8, 0:128] = value * A1[4 + i, 6, 0:8, 0:128]
+        E1[4 + i, 1, 0:8, 0:128] = value * own1[i]
 
     coarsen0(resid0, put_b1)
     pack1(1)
-    for copy in copies_c1:
-        copy.wait_send()
     copies_b1 = swap1(1, b1_s, b1_r)
 
-    xs = {0: (3, 8), 1: (9, 2), -1: (3, 2)}
+    packed = jnp.zeros((16, 128), jnp.float32)
+    for i in range(8):
+        moved = roll(VB[1 + i, 0:16, 0:128], 16 * i - 126, 1)
+        packed = jnp.where((lane16 >= 16 * i) & (lane16 < 16 * i + 4), moved, packed)
+    PKV[...] = packed
+    xs = {0: (1, 8), 1: (7, 2), -1: (1, 2)}
     xd = {0: (2, 8), 1: (0, 2), -1: (10, 2)}
     ys = {0: (0, 16), 1: (14, 2), -1: (0, 2)}
     yd = {0: (0, 16), 1: (22, 2), -1: (16, 2)}
     copies_v0 = []
     for k, (ox, oy, oz) in enumerate(CLOSE):
         if oz == 0:
-            src = E0.at[pl.ds(*xs[ox]), 0, pl.ds(*ys[oy]), lanes]
+            src = VB.at[pl.ds(*xs[ox]), pl.ds(*ys[oy]), lanes]
             dst = U0.at[pl.ds(*xd[ox]), pl.ds(*yd[oy]), lanes]
         else:
             src = PKV.at[pl.ds(*ys[oy])]
             dst = PZV.at[side_of(oz), 1 - ox, pl.ds(*yd[oy])]
         copies_v0.append(send(src, dst, v0_s.at[k], v0_r.at[k], (ox, oy, oz)))
     for i in range(8):
-        U0[2 + i, 0:16, 0:128] = E0[3 + i, 0, 0:16, 0:128]
+        U0[2 + i, 0:16, 0:128] = VB[1 + i, 0:16, 0:128]
+
+    for p in range(1, 11):
+        setup1(p)
 
     for copy in copies_cz:
         copy.wait_recv()
@@ -333,26 +361,33 @@
     par1 = (
         lax.broadcasted_iota(jnp.int32, shape1, 0) + lax.broadcasted_iota(jnp.int32, shape1, 1) // 2
     ) % 2
-    for p in range(12):
-        V1[p] = jnp.where(par1 == p % 2, E1[p, 1], 0.0)
-
-    def point1(p):
+    first1 = [jnp.where(par1 == p % 2, E1[p, 1], 0.0) for p in range(12)]
+
+    def point1(get, p):
         scaled = [A1[p, n] for n in range(6)]
-        here = V1[p]
-        return relaxed(E1[p, 1], scaled, V1[p - 1], here, V1[p + 1], 2), here
-
-    def pass1(q):
-        def body(p, carry):
-            update, here = point1(p)
-            V1[p] = jnp.where(par1 == (p + q) % 2, update, here)
-            return carry
-        return body
-
-    lax.fori_loop(1, 11, pass1(1), 0)
+        here = get(p)
+        return relaxed(E1[p, 1], scaled, get(p - 1), here, get(p + 1), 2), here
+
+    def colour1(get, store, planes, q, reach):
+        for p in planes:
+            update, here = point1(get, p)
+            mixed = jnp.where(par1 == (p + q) % 2, update, here)
+            for rows, cols in quarters(beyond_block(p - 4, 4), reach, 8, 16):
+                store(p, rows, cols, mixed[rows, cols])
+
+    def getter(ref):
+        return lambda p: ref[p]
+
+    def putter(ref):
+        def put(p, rows, cols, value):
+            ref[p, rows, cols] = value
+        return put
+
+    colour1(lambda p: first1[p], putter(V1), range(1, 11), 1, 4)
 
     def resid1(i):
-        update, here = point1(4 + i)
-        return (D1[4 + i] * (update - here))[0:8, 0:128]
+        update, here = point1(getter(V1), 4 + i)
+        return D1[i] * (update - here)[0:8, 0:128]
 
     coarsen1(resid1, 1)
     copies_fz = stage_z(1)
@@ -360,17 +395,14 @@
     for copy in copies_cm:
         copy.wait_recv()
 
-    def setup2(p, carry):
+    def setup2(p):
         here = W2[0, p]
-        weights, diagonal = faces(
-            W2[0, lax.rem(p + 15, 16)], here, W2[0, lax.rem(p + 1, 16)], 1, 0.0625
-        )
+        weights, diagonal = faces(W2[0, (p + 15) % 16], here, W2[0, (p + 1) % 16], 1, 0.0625)
         inverse = 1.0 / diagonal
         for n in range(6):
             A2[p, n] = weights[n] * inverse
         A2[p, 6] = inverse
         D2[p] = diagonal
-        return carry
 
     def coarsen2(get, store):
         for i in range(8):
@@ -386,7 +418,8 @@
     window(1)
     copies_fm = stage_xy(1)
 
-    lax.fori_loop(0, 16, setup2, 0)
+    for p in range(16):
+        setup2(p)
     coarsen2(lambda i: W2[0, i], put_c3)
     z3 = ((lane8 + 16) % 32) // 2
     for x in range(8):
@@ -412,28 +445,26 @@
     par2 = (
         lax.broadcasted_iota(jnp.int32, shape2, 0) + lax.broadcasted_iota(jnp.int32, shape2, 1)
     ) % 2
+    level2 = [W2[1, p] * A2[p, 6] for p in range(16)]
+    first2 = [jnp.where(par2 == p % 2, level2[p], 0.0) for p in range(16)]
     for p in range(16):
-        W2[1, p] = W2[1, p] * A2[p, 6]
-        V2[p] = jnp.where(par2 == p % 2, W2[1, p], 0.0)
-
-    def point2(p):
+        W2[1, p] = level2[p]
+
+    def point2(get, p):
         scaled = [A2[p, n] for n in range(6)]
-        here = V2[p]
-        before, after = V2[lax.rem(p + 15, 16)], V2[lax.rem(p + 1, 16)]
-        return relaxed(W2[1, p], scaled, before, here, after, 1), here
-
-    def pass2(q, start):
-        def body(t, carry):
-            p = lax.rem(t + start, 16)
-            update, here = point2(p)
-            V2[p] = jnp.where(par2 == (p + q) % 2, update, here)
-            return carry
-        return body
-
-    lax.fori_loop(0, 16, pass2(1, 0), 0)
+        here = get(p)
+        return relaxed(W2[1, p], scaled, get((p + 15) % 16), here, get((p + 1) % 16), 1), here
+
+    def colour2(get, ref, planes, q):
+        for t in planes:
+            p = t % 16
+            update, here = point2(get, p)
+            ref[p] = jnp.where(par2 == (p + q) % 2, update, here)
+
+    colour2(lambda p: first2[p], V2, range(16), 1)
 
     def resid2(p):
-        update, here = point2(p)
+        update, here = point2(getter(V2), p)
         return D2[p] * (update - here)
 
     def put_b3(i, value):
@@ -442,32 +473,29 @@
     coarsen2(resid2, put_b3)
 
     par3 = (sub8 + lane8 // 2 + me[0]) % 2
-    for x in range(8):
-        E3[x] = jnp.where(par3 == x % 2, B3[x], 0.0)
-
-    def pass3(q):
+    def pass3(values, q):
+        fresh = []
         for x in range(8):
             scaled = [A3[x, n] for n in range(6)]
-            here = E3[x]
-            update = relaxed(B3[x], scaled, E3[(x + 7) % 8], here, E3[(x + 1) % 8], 2)
-            E3[x] = jnp.where(par3 == (x + q) % 2, update, here)
-
-    pass3(1)
-
-    def sweep3(t, carry):
-        pass3(0)
-        pass3(1)
-        return carry
-
-    lax.fori_loop(0, CSWEEPS - 1, sweep3, 0)
-
-    for p in range(16):
-        R2[p // 2, pl.ds(0, 8, stride=2), :] = E3[p // 2]
-        R2[p // 2, pl.ds(1, 8, stride=2), :] = E3[p // 2]
-    for p in range(16):
-        V2[p] = V2[p] + R2[p // 2]
-    lax.fori_loop(0, 8, pass2(0, 13), 0)
-    lax.fori_loop(0, 6, pass2(1, 14), 0)
+            here = values[x]
+            update = relaxed(B3[x], scaled, values[(x + 7) % 8], here, values[(x + 1) % 8], 2)
+            fresh.append(jnp.where(par3 == (x + q) % 2, update, here))
+        return tuple(fresh)
+
+    solved = tuple(jnp.where(par3 == x % 2, B3[x], 0.0) for x in range(8))
+    solved = pass3(solved, 1)
+    solved = lax.fori_loop(
+        0, CSWEEPS - 1, lambda t, values: pass3(pass3(values, 0), 1), solved
+    )
+
+    for x in (6, 7, 0, 1, 2):
+        R2[x, pl.ds(0, 8, stride=2), :] = solved[x]
+        R2[x, pl.ds(1, 8, stride=2), :] = solved[x]
+    for t in range(12, 22):
+        p = t % 16
+        V2B[p] = V2[p] + R2[p // 2]
+    colour2(getter(V2B), V2C, range(13, 21), 0)
+    colour2(getter(V2C), V2B, range(14, 20), 1)
 
     wide_row = lax.broadcasted_iota(jnp.int32, (128, 256), 0)
     wide_col = lax.broadcasted_iota(jnp.int32, (128, 256), 1)
@@ -480,7 +508,7 @@
     stretch = jnp.where(wide_row == origin, 1.0, 0.0).astype(jnp.float32)
     pieces = []
     for x in range(-2, 4):
-        plane = V2[x % 16]
+        plane = V2B[x % 16]
         pieces.append(jnp.where(sub8 < 6, plane[0:8], plane[8:16]))
     spread = jnp.dot(
         jnp.concatenate(pieces, axis=0), stretch,
@@ -495,9 +523,9 @@
     for p in range(1, 11):
         x = p - 4
         add = jnp.concatenate([X1[x // 2 + 2, 0], X1[x // 2 + 2, 1]], axis=1)
-        V1[p] = V1[p] + add
-    lax.fori_loop(2, 10, pass1(0), 0)
-    lax.fori_loop(3, 9, pass1(1), 0)
+        V1B[p] = V1[p] + add
+    colour1(getter(V1B), putter(V1C), range(2, 10), 0, 3)
+    colour1(getter(V1C), putter(V1D), range(3, 9), 1, 2)
 
     for copy in copies_v0:
         copy.wait_recv()
@@ -508,41 +536,37 @@
             U0[p, :, 128:256] = roll(both, 126 - 16 * i, 1)
     sub256 = lax.broadcasted_iota(jnp.int32, (8, 256), 0)
     for j in range(6):
-        value = V1[3 + j]
+        value = V1D[3 + j]
         for half in range(2):
             piece = value[0:8, 128 * half : 128 * half + 128]
-            R0[half, pl.ds(0, 8, stride=2), :] = piece
-            R0[half, pl.ds(1, 8, stride=2), :] = piece
-        inner = jnp.concatenate([R0[0], R0[1]], axis=1)
+            X0[j, half, pl.ds(0, 8, stride=2), :] = piece
+            X0[j, half, pl.ds(1, 8, stride=2), :] = piece
+        inner = jnp.concatenate([X0[j, 0], X0[j, 1]], axis=1)
         outer = jnp.where(
             sub256 < 4,
             jnp.broadcast_to(value[8:9], (8, 256)),
             jnp.broadcast_to(value[15:16], (8, 256)),
         )
         add = jnp.concatenate([inner, outer], axis=0)
-        U0[2 * j] = U0[2 * j] + add
-        U0[2 * j + 1] = U0[2 * j + 1] + add
-
-    def point_u(p):
-        scaled = [A0[p + 1, n] for n in range(6)]
-        here = U0[p]
-        return relaxed(A0[p + 1, 6], scaled, U0[p - 1], here, U0[p + 1], 1), here
-
-    def up0(p, carry):
-        update, here = point_u(p)
-        U0[p] = jnp.where(par0 == p % 2, update, here)
-        return carry
-
-    lax.fori_loop(1, 11, up0, 0)
-
-    def last0(p, carry):
-        update, here = point_u(p)
-        out[p - 2] = jnp.where(par0 == (p + 1) % 2, update, here)[0:16, 0:128]
-        return carry
-
-    lax.fori_loop(2, 10, last0, 0)
-
-    for copies in (copies_cz, copies_b1, copies_v0, copies_cm, copies_fz, copies_fm):
+        UA[2 * j] = U0[2 * j] + add
+        UA[2 * j + 1] = U0[2 * j + 1] + add
+
+    def get_ua(p):
+        return UA[p - 1]
+
+    def get_ub(p):
+        return UB[p - 2]
+
+    def put_ub(p, rows, cols, value):
+        UB[p - 2, rows, cols] = value
+
+    def put_out(p, rows, cols, value):
+        out[p - 3] = value
+
+    colour0(get_ua, put_ub, range(2, 12), 0, 1)
+    colour0(get_ub, put_out, range(3, 11), 1, 0)
+
+    for copies in (copies_a, copies_c1, copies_cz, copies_b1, copies_v0, copies_cm, copies_fz, copies_fm):
         for copy in copies:
             copy.wait_send()
 
@@ -554,24 +578,29 @@
     dma = pltpu.SemaphoreType.DMA
     scratch = [
         vmem(14, 3, 24, 256), vmem(16, 128), vmem(2, 3, 24, 128), vmem(14, 7, 24, 256),
-        vmem(14, 24, 256), vmem(12, 24, 256), vmem(16, 128), vmem(2, 3, 24, 128), vmem(4, 16, 128),
-        vmem(12, 2, 16, 256), vmem(2, 8, 128), vmem(2, 2, 3, 16, 128), vmem(12, 7, 16, 256),
-        vmem(12, 16, 256), vmem(12, 16, 256), vmem(6, 2, 16, 128), vmem(16, 128),
+        vmem(8, 16, 128), vmem(12, 24, 256), vmem(10, 24, 256), vmem(12, 24, 256),
+        vmem(12, 24, 256), vmem(10, 24, 256), vmem(16, 128), vmem(2, 3, 24, 128),
+        vmem(4, 16, 128), vmem(6, 2, 16, 128),
+        vmem(12, 2, 16, 256), vmem(2, 8, 128), vmem(2, 2, 3, 16, 128), vmem(12, 6, 16, 256),
+        vmem(4, 8, 128), vmem(12, 16, 256), vmem(12, 16, 256), vmem(12, 16, 256),
+        vmem(12, 16, 256), vmem(6, 2, 16, 128), vmem(16, 128),
         vmem(2, 8, 128), vmem(2, 4, 8, 128), vmem(2, 2, 8, 128), vmem(2, 16, 16, 128),
-        vmem(16, 16, 128), vmem(16, 7, 16, 128), vmem(16, 16, 128), vmem(8, 16, 128),
-        vmem(8, 8, 128), vmem(8, 6, 8, 128), vmem(8, 8, 128),
-        dma((3,)), dma((26,)), dma((26,)), dma((26,)), dma((26,)), dma((26,)), dma((26,)),
+        vmem(16, 16, 128), vmem(16, 16, 128), vmem(16, 16, 128), vmem(16, 7, 16, 128),
+        vmem(16, 16, 128), vmem(8, 16, 128), vmem(8, 8, 128), vmem(8, 6, 8, 128),
+        vmem(8, 8, 128),
+        pltpu.SMEM((8, 4, 16), jnp.int32),
+        dma((4,)), dma((26,)), dma((26,)), dma((26,)), dma((26,)), dma((26,)), dma((26,)),
         dma((18,)), dma((18,)), dma((2, 4)), dma((2, 4)), dma((2, 31)), dma((2, 31)),
     ]
-    anywhere = pl.BlockSpec(memory_space=pl.ANY)
+    anywhere = pl.BlockSpec(memory_space=pltpu.HBM)
     return pl.pallas_call(
         kernel,
         out_shape=jax.ShapeDtypeStruct(source_term.shape, jnp.float32),
-        in_specs=[anywhere, anywhere, anywhere, pl.BlockSpec(memory_space=pltpu.SMEM)],
+        in_specs=[anywhere, anywhere, anywhere, anywhere],
         out_specs=pl.BlockSpec(memory_space=pltpu.VMEM),
         scratch_shapes=scratch,
         compiler_params=pltpu.CompilerParams(
-            collective_id=0, has_side_effects=True, vmem_limit_bytes=40 << 20
+            collective_id=0, has_side_effects=True, vmem_limit_bytes=60 << 20
         ),
     )(source_term, conductivity, initial_guess, box_owner)
 

time: 62.4 us -> 51.2 us (0.82)
  Pallas kernels: 58.2 us -> 48.9 us
  local copies, waits for them, and re-layouts: 3.87 us -> 1.47 us
    pallas_call x1, Pallas kernels: 58.2 us -> 48.9 us  [local(): pl.pallas_call(kernel, out_shape=jax.ShapeDtypeStruct(source_term.shape,...]
    unnamed x9 -> x1, local copies, waits for them, and re-layouts: 3.87 us -> 1.47 us
where the time goes in v2:
time: 51.2 us; the launch traced here: 50.3 us
  Pallas kernels  48.9 us (96%)
  local copies, waits for them, and re-layouts  1.47 us (3%)
    pallas_call x1, Pallas kernels, local(): pl.pallas_call(kernel, out_shape=jax.ShapeDtypeStruct(source_term.shape,...  48.9 us
    unnamed x1, local copies, waits for them, and re-layouts  1.47 us

profile of v2, /device:TPU:1, one launch (start us, length us, event | category | flops | bytes accessed | tf_op | source)
XLA Modules:
  0.0 50.3 jit_solution(6120072904980815270)
XLA Ops:
  0.0 48.9 %shard_map.46 = f32[8,16,128]{2,1,0:T(8,128)} custom-call(f32[8,16,128]{2,1,0:T(8,128)} %f_in.1, f32[8,16,128]{2,1,0:T(8,128)} %c_in.1, f32[8,16,128]{2,1,0:T(8,128)} %v_in.1, s32[8,4,16]{2,1,0:T(4,128)} %owner_in.1), custom_call_target="tpu_custom_call" | custom-call | tf_op jit(solution)/shard_map/pallas_call | solution.py:596
  48.9 1.5 %copy.6 = f32[8,16,128]{2,1,0:T(8,128)} copy(f32[8,16,128]{2,1,0:T(8,128)} %shard_map.46) | data formatting | bytes 131072

commit v3 on v2

--- a/solution.py
+++ b/solution.py
@@ -78,7 +78,7 @@
 def kernel(
     f_in, c_in, v_in, owner_in, out,
     E0, PK0, PZ0, A0, D0, VA, VB, U0, UA, UB, PKV, PZV, R0, X0,
-    E1, PK1, PZ1, A1, D1, V1, V1B, V1C, V1D, X1, R1,
+    C1, E1, PK1, PZ1, A1, D1, V1, V1B, V1C, V1D, X1, R1,
     T2, ZR, S2, W2, V2, V2B, V2C, A2, D2, R2, E3, A3, B3, owner,
     in_sem, a_s, a_r, c1_s, c1_r, b1_s, b1_r, v0_s, v0_r, z_s, z_r, m_s, m_r,
 ):
@@ -155,24 +155,39 @@
 
     pl.semaphore_wait(barrier, len(others))
 
-    x_from = {0: (3, 8), 1: (8, 3), -1: (3, 3)}
-    x_to = {0: (3, 8), 1: (0, 3), -1: (11, 3)}
-    y_from = {0: (0, 16), 1: (13, 3), -1: (0, 3)}
-    y_to = {0: (0, 16), 1: (21, 3), -1: (16, 3)}
-    lanes = pl.ds(0, 128)
-
     def side_of(oz):
         return 0 if oz == -1 else 1
 
+    def reach0(offset, width, count, low, high):
+        if offset == 0:
+            return (low, count), (low, count)
+        if offset == 1:
+            return (low + count - width, width), (high - width, width)
+        return (low, width), (low + count, width)
+
+    lanes = pl.ds(0, 128)
+
     copies_a = []
     for k, (ox, oy, oz) in enumerate(NEAR):
+        width = 4 - abs(ox) - abs(oy) - abs(oz)
+        (ys, yc), (yd, _) = reach0(oy, width, 16, 0, 24)
         if oz == 0:
-            src = E0.at[pl.ds(*x_from[ox]), :, pl.ds(*y_from[oy]), lanes]
-            dst = E0.at[pl.ds(*x_to[ox]), :, pl.ds(*y_to[oy]), lanes]
+            (xs, xc), _ = reach0(ox, width, 8, 3, 3)
+            xd = {0: 3, 1: 3 - width, -1: 11}[ox]
+            parts = [(0, 3, xs, xc, xd, ys, yc, yd)]
+            if width == 3:
+                (ys2, yc2), (yd2, _) = reach0(oy, 2, 16, 0, 24)
+                (xs2, xc2), _ = reach0(ox, 2, 8, 3, 3)
+                xd2 = {0: 3, 1: 1, -1: 11}[ox]
+                parts = [(0, 2, xs, xc, xd, ys, yc, yd), (2, 1, xs2, xc2, xd2, ys2, yc2, yd2)]
+            for j, (n, count, xs, xc, xd, ys, yc, yd) in enumerate(parts):
+                src = E0.at[pl.ds(xs, xc), pl.ds(n, count), pl.ds(ys, yc), lanes]
+                dst = E0.at[pl.ds(xd, xc), pl.ds(n, count), pl.ds(yd, yc), lanes]
+                copies_a.append(send(src, dst, a_s.at[k, j], a_r.at[k, j], (ox, oy, oz)))
         else:
-            src = PK0.at[pl.ds(*y_from[oy])]
-            dst = PZ0.at[side_of(oz), 1 - ox, pl.ds(*y_to[oy])]
-        copies_a.append(send(src, dst, a_s.at[k], a_r.at[k], (ox, oy, oz)))
+            src = PK0.at[pl.ds(ys, yc)]
+            dst = PZ0.at[side_of(oz), 1 - ox, pl.ds(yd, yc)]
+            copies_a.append(send(src, dst, a_s.at[k, 0], a_r.at[k, 0], (ox, oy, oz)))
 
     def swap1(kind, send_sem, recv_sem):
         xd = {0: 4, 1: 0, -1: 8}
@@ -214,8 +229,8 @@
             copies.append(send(src, dst, m_s.at[kind, k], m_r.at[kind, k], (ox, oy, 0)))
         return copies
 
+    copies_cz = stage_z(0)
     copies_c1 = swap1(0, c1_s, c1_r)
-    copies_cz = stage_z(0)
 
     sub8 = lax.broadcasted_iota(jnp.int32, (8, 128), 0)
     labels = []
@@ -293,17 +308,12 @@
         update, here = point0(get_vb, 3 + i)
         return D0[i] * (update - here)[0:16, 0:128]
 
-    for copy in copies_c1:
-        copy.wait_recv()
-
     def unpack1(kind):
         lane_16 = lax.broadcasted_iota(jnp.int32, (16, 128), 1)
         for dx in range(3):
             both = jnp.where(lane_16 % 16 < 8, PZ1[kind, 1, dx], PZ1[kind, 0, dx])
             for i in range(4):
                 E1[4 * dx + i, kind, :, 128:256] = roll(both, 120 - 16 * i, 1)
-
-    unpack1(0)
 
     def setup1(p):
         weights, diagonal = faces(E1[p - 1, 0], E1[p, 0], E1[p + 1, 0], 2, 0.25)
@@ -313,9 +323,26 @@
         if 4 <= p < 8:
             D1[p - 4] = diagonal[0:8, 0:128]
 
+    near1 = []
+    sub256 = lax.broadcasted_iota(jnp.int32, (8, 256), 0)
+    for i in range(6):
+        both = pair_sum(E0[2 * i + 1, 1] + E0[2 * i + 2, 1])
+        for half in range(2):
+            C1[i, half] = both[:, 128 * half : 128 * half + 128]
+        rows = []
+        for first, count in ((0, 8), (16, 1), (22, 1)):
+            if count == 8:
+                halves = [C1[i, h, pl.ds(0, 8, stride=2), :] + C1[i, h, pl.ds(1, 8, stride=2), :] for h in range(2)]
+                rows.append(jnp.concatenate(halves, axis=1))
+            else:
+                rows.append(jnp.broadcast_to(both[first : first + 1] + both[first + 1 : first + 2], (8, 256)))
+        near1.append(
+            0.125 * jnp.concatenate([rows[0], jnp.where(sub256 < 4, rows[1], rows[2])], axis=0)
+        )
     own1 = []
-    for p in range(4, 8):
-        own1.append(1.0 / faces(E1[p - 1, 0], E1[p, 0], E1[p + 1, 0], 2, 0.25)[1][0:8, 0:128])
+    for i in range(4):
+        diagonal = faces(near1[i], near1[i + 1], near1[i + 2], 2, 0.25)[1]
+        own1.append(1.0 / diagonal[0:8, 0:128])
 
     def put_b1(i, value):
         E1[4 + i, 1, 0:8, 0:128] = value * own1[i]
@@ -345,6 +372,9 @@
     for i in range(8):
         U0[2 + i, 0:16, 0:128] = VB[1 + i, 0:16, 0:128]
 
+    for copy in copies_c1:
+        copy.wait_recv()
+    unpack1(0)
     for p in range(1, 11):
         setup1(p)
 
@@ -534,7 +564,6 @@
         for p in {0: range(0, 2), 1: range(2, 10), 2: range(10, 12)}[dx]:
             i = {0: p + 6, 1: p - 2, 2: p - 10}[dx]
             U0[p, :, 128:256] = roll(both, 126 - 16 * i, 1)
-    sub256 = lax.broadcasted_iota(jnp.int32, (8, 256), 0)
     for j in range(6):
         value = V1D[3 + j]
         for half in range(2):
@@ -581,7 +610,7 @@
         vmem(8, 16, 128), vmem(12, 24, 256), vmem(10, 24, 256), vmem(12, 24, 256),
         vmem(12, 24, 256), vmem(10, 24, 256), vmem(16, 128), vmem(2, 3, 24, 128),
         vmem(4, 16, 128), vmem(6, 2, 16, 128),
-        vmem(12, 2, 16, 256), vmem(2, 8, 128), vmem(2, 2, 3, 16, 128), vmem(12, 6, 16, 256),
+        vmem(6, 2, 24, 128), vmem(12, 2, 16, 256), vmem(2, 8, 128), vmem(2, 2, 3, 16, 128), vmem(12, 6, 16, 256),
         vmem(4, 8, 128), vmem(12, 16, 256), vmem(12, 16, 256), vmem(12, 16, 256),
         vmem(12, 16, 256), vmem(6, 2, 16, 128), vmem(16, 128),
         vmem(2, 8, 128), vmem(2, 4, 8, 128), vmem(2, 2, 8, 128), vmem(2, 16, 16, 128),
@@ -589,7 +618,7 @@
         vmem(16, 16, 128), vmem(8, 16, 128), vmem(8, 8, 128), vmem(8, 6, 8, 128),
         vmem(8, 8, 128),
         pltpu.SMEM((8, 4, 16), jnp.int32),
-        dma((4,)), dma((26,)), dma((26,)), dma((26,)), dma((26,)), dma((26,)), dma((26,)),
+        dma((4,)), dma((26, 2)), dma((26, 2)), dma((26,)), dma((26,)), dma((26,)), dma((26,)),
         dma((18,)), dma((18,)), dma((2, 4)), dma((2, 4)), dma((2, 31)), dma((2, 31)),
     ]
     anywhere = pl.BlockSpec(memory_space=pltpu.HBM)
@@ -600,7 +629,7 @@
         out_specs=pl.BlockSpec(memory_space=pltpu.VMEM),
         scratch_shapes=scratch,
         compiler_params=pltpu.CompilerParams(
-            collective_id=0, has_side_effects=True, vmem_limit_bytes=60 << 20
+            collective_id=0, has_side_effects=True, vmem_limit_bytes=55120 << 10
         ),
     )(source_term, conductivity, initial_guess, box_owner)
 

time: 51.2 us -> 49.2 us (0.961); the launches traced: 50.3 us -> 49 us
  Pallas kernels: 48.9 us -> 47.7 us
    pallas_call x1, Pallas kernels: 48.9 us -> 47.7 us  [local(): pl.pallas_call(kernel, out_shape=jax.ShapeDtypeStruct(source_term.shape,...]
    unnamed x1 -> x3, local copies, waits for them, and re-layouts: 1.47 us -> 1.35 us
where the time goes in v3:
time: 49.2 us; the launch traced here: 49 us
  Pallas kernels  47.7 us (97%)
  local copies, waits for them, and re-layouts  1.35 us (3%)
    pallas_call x1, Pallas kernels, local(): pl.pallas_call(kernel, out_shape=jax.ShapeDtypeStruct(source_term.shape,...  47.7 us
    unnamed x3, local copies, waits for them, and re-layouts  1.35 us

profile of v3, /device:TPU:1, one launch (start us, length us, event | category | flops | bytes accessed | tf_op | source)
XLA Modules:
  0.0 49.0 jit_solution(11155828583854314243)
XLA Ops:
  0.0 0.0 copy-start
  0.0 0.7 %copy-done = s32[8,4,16]{2,1,0:T(4,128)S(1)} copy-done((s32[8,4,16]{2,1,0:T(4,128)S(1)}, s32[8,4,16]{2,1,0:T(4,128)}, u32[]{:S(2)}) %copy-start) | copy-done | bytes 2072
  0.7 47.7 %shard_map.46 = f32[8,16,128]{2,1,0:T(8,128)S(1)} custom-call(f32[8,16,128]{2,1,0:T(8,128)} %f_in.1, f32[8,16,128]{2,1,0:T(8,128)} %c_in.1, f32[8,16,128]{2,1,0:T(8,128)} %v_in.1, s32[8,4,16]{2,1,0:T(4,128)S(1)} %copy-done), custom_call_target="tpu_custom_call" | custom-call | tf_op jit(solution)/shard_map/pallas_call | solution.py:625
  48.4 0.6 %copy.6 = f32[8,16,128]{2,1,0:T(8,128)} copy(f32[8,16,128]{2,1,0:T(8,128)S(1)} %shard_map.46) | data formatting | bytes 131072
Async XLA Ops:
  0.0 0.7 %copy-start = (s32[8,4,16]{2,1,0:T(4,128)S(1)}, s32[8,4,16]{2,1,0:T(4,128)}, u32[]{:S(2)}) copy-start(s32[8,4,16]{2,1,0:T(4,128)} %owner_in.1) | copy-start | bytes 6148

commit v4 on v3

--- a/solution.py
+++ b/solution.py
@@ -13,6 +13,7 @@
 screening = 0.05
 
 NEAR = [d for d in itertools.product((-1, 0, 1), repeat=3) if d != (0, 0, 0)]
+NEAR.sort(key=lambda d: (-2 * abs(d[1]) - abs(d[0]) - abs(d[2]) / 2, d))
 CLOSE = [d for d in NEAR if abs(d[0]) + abs(d[1]) + abs(d[2]) <= 2]
 PLANE = [d for d in itertools.product(range(SX), range(SY)) if d != (0, 0)]
 ALONG = [-2, -1, 1, 2]
@@ -135,15 +136,11 @@
             tile = jnp.where((lane8 >= 16 * i) & (lane8 < 16 * i + 16), moved, tile)
         PK1[kind] = tile
 
-    row_of = lax.broadcasted_iota(jnp.int32, (128, 128), 0)
-    col_of = lax.broadcasted_iota(jnp.int32, (128, 128), 1)
-    squeeze = jnp.where(row_of // 4 == (col_of + 16) % 32, 0.25, 0.0).astype(jnp.float32)
-
     def coarsen1(get, kind):
         both = jnp.concatenate([get(0) + get(1), get(2) + get(3)], axis=0)
-        R1[...] = jnp.dot(
-            both, squeeze, precision=lax.Precision.HIGHEST, preferred_element_type=jnp.float32
-        )
+        pairs = pair_sum(both)
+        quads = pairs + jnp.where(lane16 % 4 < 2, roll(pairs, -2, 1), roll(pairs, 2, 1))
+        R1[...] = 0.25 * jnp.take_along_axis(quads, 4 * ((lane16 + 16) % 32), axis=1)
         T2[kind] = 0.25 * (R1[pl.ds(0, 8, stride=2), :] + R1[pl.ds(1, 8, stride=2), :])
 
     def put_c1(i, value):
@@ -527,27 +524,15 @@
     colour2(getter(V2B), V2C, range(13, 21), 0)
     colour2(getter(V2C), V2B, range(14, 20), 1)
 
-    wide_row = lax.broadcasted_iota(jnp.int32, (128, 256), 0)
-    wide_col = lax.broadcasted_iota(jnp.int32, (128, 256), 1)
-    beyond = wide_col - 128
-    origin = jnp.where(
-        wide_col < 128,
-        48 + wide_col // 4,
-        jnp.where(beyond < 64, 80 + beyond // 4, 16 + beyond // 4),
-    )
-    stretch = jnp.where(wide_row == origin, 1.0, 0.0).astype(jnp.float32)
+    own_lane = 48 + lane8 // 4
+    halo_lane = jnp.where(lane8 < 64, 80 + lane8 // 4, 16 + lane8 // 4)
     pieces = []
     for x in range(-2, 4):
         plane = V2B[x % 16]
         pieces.append(jnp.where(sub8 < 6, plane[0:8], plane[8:16]))
-    spread = jnp.dot(
-        jnp.concatenate(pieces, axis=0), stretch,
-        precision=lax.Precision.HIGHEST, preferred_element_type=jnp.float32,
-    )
     for x in range(6):
-        part = spread[8 * x : 8 * x + 8]
-        for half in range(2):
-            piece = part[:, 128 * half : 128 * half + 128]
+        for half, source in enumerate((own_lane, halo_lane)):
+            piece = jnp.take_along_axis(pieces[x], source, axis=1)
             X1[x, half, pl.ds(0, 8, stride=2), :] = piece
             X1[x, half, pl.ds(1, 8, stride=2), :] = piece
     for p in range(1, 11):

time: 49.2 us -> 47.6 us (0.967)
  Pallas kernels: 47.7 us -> 45.6 us
    pallas_call x1, Pallas kernels: 47.7 us -> 45.6 us  [local(): pl.pallas_call(kernel, out_shape=jax.ShapeDtypeStruct(source_term.shape,...]
where the time goes in v4:
time: 47.6 us; the launch traced here: 47 us
  Pallas kernels  45.6 us (96%)
  local copies, waits for them, and re-layouts  1.35 us (3%)
    pallas_call x1, Pallas kernels, local(): pl.pallas_call(kernel, out_shape=jax.ShapeDtypeStruct(source_term.shape,...  45.6 us
    unnamed x3, local copies, waits for them, and re-layouts  1.35 us

profile of v4, /device:TPU:1, one launch (start us, length us, event | category | flops | bytes accessed | tf_op | source)
XLA Modules:
  0.0 47.0 jit_solution(7901265337645614299)
XLA Ops:
  0.0 0.0 copy-start
  0.0 0.7 %copy-done = s32[8,4,16]{2,1,0:T(4,128)S(1)} copy-done((s32[8,4,16]{2,1,0:T(4,128)S(1)}, s32[8,4,16]{2,1,0:T(4,128)}, u32[]{:S(2)}) %copy-start) | copy-done | bytes 2072
  0.7 45.6 %shard_map.46 = f32[8,16,128]{2,1,0:T(8,128)S(1)} custom-call(f32[8,16,128]{2,1,0:T(8,128)} %f_in.1, f32[8,16,128]{2,1,0:T(8,128)} %c_in.1, f32[8,16,128]{2,1,0:T(8,128)} %v_in.1, s32[8,4,16]{2,1,0:T(4,128)S(1)} %copy-done), custom_call_target="tpu_custom_call" | custom-call | tf_op jit(solution)/shard_map/pallas_call | solution.py:610
  46.4 0.6 %copy.6 = f32[8,16,128]{2,1,0:T(8,128)} copy(f32[8,16,128]{2,1,0:T(8,128)S(1)} %shard_map.46) | data formatting | bytes 131072
Async XLA Ops:
  0.0 0.7 %copy-start = (s32[8,4,16]{2,1,0:T(4,128)S(1)}, s32[8,4,16]{2,1,0:T(4,128)}, u32[]{:S(2)}) copy-start(s32[8,4,16]{2,1,0:T(4,128)} %owner_in.1) | copy-start | bytes 6148

commit v5 on v4

--- a/solution.py
+++ b/solution.py
@@ -16,6 +16,7 @@
 NEAR.sort(key=lambda d: (-2 * abs(d[1]) - abs(d[0]) - abs(d[2]) / 2, d))
 CLOSE = [d for d in NEAR if abs(d[0]) + abs(d[1]) + abs(d[2]) <= 2]
 PLANE = [d for d in itertools.product(range(SX), range(SY)) if d != (0, 0)]
+PLANE.sort(key=lambda d: (-min(d[0], SX - d[0]) - 2 * min(d[1], SY - d[1]), d))
 ALONG = [-2, -1, 1, 2]
 
 
@@ -23,7 +24,7 @@
     found = {(a % SX, b % SY, c % SZ) for a, b, c in NEAR}
     found |= {(a, b, 0) for a, b in PLANE}
     found |= {(0, 0, c % SZ) for c in ALONG}
-    return sorted(found)
+    return sorted(found, key=lambda d: (-2 * min(d[1], SY - d[1]) - min(d[0], SX - d[0]) - min(d[2], SZ - d[2]), d))
 
 
 def roll(values, shift, axis):

time: 47.6 us -> 47.5 us (level)
  no operation moved by 1% of the time
where the time goes in v5:
time: 47.5 us; the launch traced here: 46.7 us
  Pallas kernels  45.4 us (96%)
  local copies, waits for them, and re-layouts  1.35 us (3%)
    pallas_call x1, Pallas kernels, local(): pl.pallas_call(kernel, out_shape=jax.ShapeDtypeStruct(source_term.shape,...  45.4 us
    unnamed x3, local copies, waits for them, and re-layouts  1.35 us

profile of v5, /device:TPU:1, one launch (start us, length us, event | category | flops | bytes accessed | tf_op | source)
XLA Modules:
  0.0 46.7 jit_solution(8807387914038656637)
XLA Ops:
  0.0 0.0 copy-start
  0.0 0.7 %copy-done = s32[8,4,16]{2,1,0:T(4,128)S(1)} copy-done((s32[8,4,16]{2,1,0:T(4,128)S(1)}, s32[8,4,16]{2,1,0:T(4,128)}, u32[]{:S(2)}) %copy-start) | copy-done | bytes 2072
  0.7 45.4 %shard_map.46 = f32[8,16,128]{2,1,0:T(8,128)S(1)} custom-call(f32[8,16,128]{2,1,0:T(8,128)} %f_in.1, f32[8,16,128]{2,1,0:T(8,128)} %c_in.1, f32[8,16,128]{2,1,0:T(8,128)} %v_in.1, s32[8,4,16]{2,1,0:T(4,128)S(1)} %copy-done), custom_call_target="tpu_custom_call" | custom-call | tf_op jit(solution)/shard_map/pallas_call | solution.py:611
  46.1 0.6 %copy.6 = f32[8,16,128]{2,1,0:T(8,128)} copy(f32[8,16,128]{2,1,0:T(8,128)S(1)} %shard_map.46) | data formatting | bytes 131072
Async XLA Ops:
  0.0 0.7 %copy-start = (s32[8,4,16]{2,1,0:T(4,128)S(1)}, s32[8,4,16]{2,1,0:T(4,128)}, u32[]{:S(2)}) copy-start(s32[8,4,16]{2,1,0:T(4,128)} %owner_in.1) | copy-start | bytes 6148
